TPU v7x, 128 devices: a whole 4x4x4 slice. The times are simulated.
128 devices in a mesh: space: 8 (over y, core), terms: 16 (over x, z).
Axes of the slice: x: 4, y: 4, z: 4, core: 2. Of those that a mesh axis runs over, the one named last changes fastest.
Arguments:
- forcing: float32 [176, 3, 16, 32, 128], P('terms', None, 'space'), may hold values from -6 to 6
- stencil: float32 [27, 3, 3], replicated, may hold values from -0.12 to 3, as said below
- fields: float32 [5, 16, 32, 128], P(None, 'space'), may hold values from -3 to 3
- coupling: float32 [126, 5], replicated, may hold values from 0.25 to 1
- slot_term: int32 [176], replicated, may hold values from -1 to 125, as said below
Outputs:
- solution: float32 [176, 3, 16, 32, 128], P('terms', None, 'space')
Inputs may be any that keep to these rules, and one draw needn't show every extreme that they name: `slot_term`: device k of terms holds the slots k * 11 to (k + 1) * 11 - 1; of these, the first 1 hold level-0 terms or -1, the next 1 level 1, then 1 level 2, 3 level 3 and 5 level 4. Every term stands in exactly one slot. The central diagonal entries stencil[13, a, a] lie in 2 to 3; every other entry lies in -0.12 to 0.05.
All inputs are finite; a program needn't handle non-finite values.
Results may differ from a plain program's by a relative error of at most 0.00014.
Values sent between devices are 32-bit elements; how exact they have to be, the bound alone decides.
A program may use at most 128 MiB of HBM per device.

v0:
```python
import math

import jax
import jax.numpy as jnp
import numpy as np
from jax import lax
from jax.sharding import PartitionSpec as P

DIMS = 5
DEGREE = 4
TERMS = 126


def with_halo(cells, sides, width):
    for axis, dim in sides:
        count = lax.axis_size(axis)
        ends = count - 1
        head = lax.slice_in_dim(cells, 0, width, axis=dim)
        tail = lax.slice_in_dim(cells, cells.shape[dim] - width, cells.shape[dim], axis=dim)
        cells = jnp.concatenate(
            [
                lax.ppermute(tail, axis, [(i, (i + 1) % count) for i in range(ends)]),
                cells,
                lax.ppermute(head, axis, [((i + 1) % count, i) for i in range(ends)]),
            ],
            axis=dim,
        )
    return cells


def compositions(total, pieces_left):
    if pieces_left == 1:
        return [[total]]
    result = []
    for leading in range(total, -1, -1):
        for remainder in compositions(total - leading, pieces_left - 1):
            result.append([leading] + remainder)
    return result


def chaos_parents(dimensions, top_degree):
    indices = []
    for level_now in range(top_degree + 1):
        indices.extend(compositions(level_now, dimensions))
    lookup = {}
    for number, vector in enumerate(indices):
        lookup[tuple(vector)] = number
    parents = np.full((len(indices), dimensions), -1, dtype=np.int32)
    for number, vector in enumerate(indices):
        for dimension in range(dimensions):
            if vector[dimension] > 0:
                lowered = list(vector)
                lowered[dimension] -= 1
                parents[number, dimension] = lookup[tuple(lowered)]
    return parents


def shifted(array, offset, axis_dim):
    if offset == 0:
        return array
    length = array.shape[axis_dim]
    zeros_edge = jnp.zeros_like(lax.slice_in_dim(array, 0, 1, axis=axis_dim))
    if offset > 0:
        return jnp.concatenate(
            [lax.slice_in_dim(array, 1, length, axis=axis_dim), zeros_edge], axis=axis_dim
        )
    return jnp.concatenate(
        [zeros_edge, lax.slice_in_dim(array, 0, length - 1, axis=axis_dim)], axis=axis_dim
    )


def apply_stencil(extended, stencil):
    inner_x = extended.shape[2] - 2
    summed = jnp.zeros(extended.shape[:2] + (inner_x,) + extended.shape[3:], jnp.float32)
    for step_y in range(3):
        for step_z in range(3):
            moved_yz = shifted(shifted(extended, step_y - 1, 3), step_z - 1, 4)
            for step_x in range(3):
                window = lax.slice_in_dim(moved_yz, step_x, step_x + inner_x, axis=2)
                block_coef = stencil[9 * step_x + 3 * step_y + step_z]
                summed = summed + jnp.einsum(
                    "ab,sbxyz->saxyz", block_coef, window, precision=lax.Precision.HIGHEST
                )
    return summed


def on_device(forcing, stencil, fields, coupling, slot_term):
    groups = lax.axis_size("terms")
    slot_dev = forcing.shape[0]
    my_group = lax.axis_index("terms")
    parents = chaos_parents(DIMS, DEGREE)
    level_counts = [math.comb(level_now + DIMS - 1, DIMS - 1) for level_now in range(DEGREE + 1)]
    level_caps = [(level_count + groups - 1) // groups for level_count in level_counts]
    level_starts = [sum(level_caps[:level_now]) for level_now in range(DEGREE + 1)]
    all_terms = slot_term.reshape(groups, slot_dev)
    my_terms = lax.dynamic_slice_in_dim(slot_term, my_group * slot_dev, slot_dev)
    pivots = jnp.diagonal(stencil[13])[None, :, None, None, None]
    link_mask = parents[:, :, None] == np.arange(TERMS)[None, None, :]
    link_table = jnp.where(jnp.asarray(link_mask), coupling[:, :, None], 0.0)
    term_range = jnp.arange(TERMS, dtype=jnp.int32)

    def rim_one(field):
        return with_halo(field, (("space", 2),), 1)

    def relax(level_load, need_image):
        first_pass = level_load / pivots
        settled = first_pass + (level_load - apply_stencil(rim_one(first_pass), stencil)) / pivots
        if need_image:
            return (settled, apply_stencil(rim_one(settled), stencil))
        return (settled, None)

    blocks = []
    begin_level = 0
    prev_image = None
    for level_now in range(begin_level, DEGREE + 1):
        level_start = level_starts[level_now]
        level_cap = level_caps[level_now]
        child_ids = my_terms[level_start : level_start + level_cap]
        filled = (child_ids >= 0).astype(jnp.float32)[:, None, None, None, None]
        level_load = forcing[level_start : level_start + level_cap]
        if level_now == 0:
            level_load = level_load * filled
        else:
            prev_start = level_starts[level_now - 1]
            prev_cap = level_caps[level_now - 1]
            parent_ids = all_terms[:, prev_start : prev_start + prev_cap].reshape(-1)
            empty_sum = jnp.zeros((level_cap,) + forcing.shape[1:], jnp.float32)
            piece = lax.all_gather(prev_image, "terms", axis=0, tiled=True)
            fold_row_ids = lax.slice_in_dim(parent_ids, 0, piece.shape[0], axis=0)
            child_hot = (child_ids[:, None] == term_range[None, :]).astype(jnp.float32)
            row_hot = (fold_row_ids[:, None] == term_range[None, :]).astype(jnp.float32)
            mixture = jnp.einsum(
                "cdr,raxyz->cdaxyz",
                jnp.einsum(
                    "ct,tdq,rq->cdr",
                    child_hot,
                    link_table,
                    row_hot,
                    precision=lax.Precision.HIGHEST,
                ),
                piece,
                precision=lax.Precision.HIGHEST,
            )
            contribution = empty_sum + jnp.sum(mixture * fields[None, :, None], axis=1)
            level_load = (level_load - contribution) * filled
        settled, level_image = relax(level_load, level_now < DEGREE)
        blocks.append(settled)
        prev_image = level_image
    return jnp.concatenate(blocks, axis=0)


def solution(mesh):
    return jax.shard_map(
        on_device,
        mesh=mesh,
        in_specs=(
            P("terms", None, "space", None, None),
            P(),
            P(None, "space", None, None),
            P(),
            P(),
        ),
        out_specs=P("terms", None, "space", None, None),
        check_vma=False,
    )
```

profile of v0, /device:TPU:1, one launch (start us, length us, event | category | flops | bytes accessed | tf_op | source)
XLA Modules:
  0.0 470.6 jit_solution(8094971979689062714)
XLA Ops:
  11.6 4.6 collective-permute-start
  16.2 1.9 collective-permute-start.1
  18.8 3.0 collective-permute-done.1
  34.8 2.6 collective-permute-start.3
  37.7 2.6 collective-permute-done.3
  54.3 42.0 %all-gather.5.cloned.1.call-done = f32[16,3,2,32,128]{4,3,2,1,0:T(8,128)} async-done(((f32[1,3,2,32,128]{4,3,2,1,0:T(8,128)}), f32[16,3,2,32,128]{4,3,2,1,0:T(8,128)}) %all-gather.5.cloned.1.call-update) | async-done | bytes 1572880 | tf_op jit(solution)/shard_map/all_gather | solution.py:128
  96.3 3.3 fusion.41
  99.7 4.9 %collective-permute-start.4 = (f32[1,3,1,32,128]{4,1,3,2,0:T(4,128)S(1)}, f32[1,3,1,32,128]{4,1,3,2,0:T(4,128)S(1)}, u32[]{:S(2)}, u32[]{:S(2)}) collective-permute-start(f32[1,3,1,32,128]{4,1,3,2,0:T(4,128)S(1)} %get-tuple-element.122), channel_id=1, source_target_pairs={{0,16},{16,32},{32,48},{48,64},{64,80},{80,96},{96,112},{1,17},{17... | collective-permute-start | bytes 147464 | tf_op jit(solution)/shard_map/ppermute | solution.py:22
  104.7 2.3 collective-permute-start.5
  107.4 2.9 collective-permute-done.5
  123.4 2.6 collective-permute-start.7
  126.3 2.6 collective-permute-done.7
  142.4 39.4 %all-gather.7.cloned.1.call-done = f32[16,3,2,32,128]{4,3,2,1,0:T(8,128)} async-done(((f32[1,3,2,32,128]{4,3,2,1,0:T(8,128)}), f32[16,3,2,32,128]{4,3,2,1,0:T(8,128)}) %all-gather.7.cloned.1.call-update) | async-done | bytes 1572880 | tf_op jit(solution)/shard_map/all_gather | solution.py:128
  181.7 3.3 fusion.38
  185.2 4.9 %collective-permute-start.8 = (f32[1,3,1,32,128]{4,1,3,2,0:T(4,128)S(1)}, f32[1,3,1,32,128]{4,1,3,2,0:T(4,128)S(1)}, u32[]{:S(2)}, u32[]{:S(2)}) collective-permute-start(f32[1,3,1,32,128]{4,1,3,2,0:T(4,128)S(1)} %get-tuple-element.118), channel_id=1, source_target_pairs={{0,16},{16,32},{32,48},{48,64},{64,80},{80,96},{96,112},{1,17},{17... | collective-permute-start | bytes 147464 | tf_op jit(solution)/shard_map/ppermute | solution.py:22
  190.1 2.3 collective-permute-start.9
  192.8 2.9 collective-permute-done.9
  208.8 2.6 collective-permute-start.11
  211.8 2.6 collective-permute-done.11
  226.8 40.4 %all-gather.9.cloned.1.call-done = f32[16,3,2,32,128]{4,3,2,1,0:T(8,128)} async-done(((f32[1,3,2,32,128]{4,3,2,1,0:T(8,128)}), f32[16,3,2,32,128]{4,3,2,1,0:T(8,128)}) %all-gather.9.cloned.1.call-update) | async-done | bytes 1572880 | tf_op jit(solution)/shard_map/all_gather | solution.py:128
  267.2 4.9 %multiply_reduce_fusion.1 = f32[3,3,2,32,128]{4,3,2,1,0:T(8,128)S(1)} fusion(f32[16,3,2,32,128]{4,3,2,1,0:T(8,128)} %all-gather.9.cloned.1.call-done, f32[5,2,32,128]{3,0,2,1:T(8,128)S(1)} %copy.37, f32[3,5,16,1,1,1]{2,0,1,5,4,3:T(4,128)S(1)} %convolution_bitcast_fusion.97), kind=kOutput, calls=%fused_computation.5 | convolution fusion | flops 71442432 | bytes 2032576 | tf_op jit(solution)/shard_map/cdr,raxyz->cdaxyz/dot_general | solution.py:132
  272.6 4.9 %collective-permute-start.12 = (f32[3,3,1,32,128]{4,1,3,2,0:T(4,128)S(1)}, f32[3,3,1,32,128]{4,1,3,2,0:T(4,128)S(1)}, u32[]{:S(2)}, u32[]{:S(2)}) collective-permute-start(f32[3,3,1,32,128]{4,1,3,2,0:T(4,128)S(1)} %get-tuple-element.66), channel_id=1, source_target_pairs={{0,16},{16,32},{32,48},{48,64},{64,80},{80,96},{96,112},{1,17},{17... | collective-permute-start | bytes 442376 | tf_op jit(solution)/shard_map/ppermute | solution.py:22
  277.5 2.3 collective-permute-start.13
  280.7 3.8 collective-permute-done.13
  312.5 2.4 collective-permute-start.15
  315.7 3.8 collective-permute-done.15
  346.3 51.4 %all-gather.11.cloned.1.call-done = f32[48,3,2,32,128]{4,3,2,1,0:T(8,128)} async-done(((f32[3,3,2,32,128]{4,3,2,1,0:T(8,128)}), f32[48,3,2,32,128]{4,3,2,1,0:T(8,128)}) %all-gather.11.cloned.1.call-update) | async-done | bytes 4718608 | tf_op jit(solution)/shard_map/all_gather | solution.py:128
  397.7 10.5 %multiply_reduce_fusion = f32[5,3,2,32,128]{4,3,2,1,0:T(8,128)S(1)} fusion(f32[48,3,2,32,128]{4,3,2,1,0:T(8,128)} %all-gather.11.cloned.1.call-done, f32[5,2,32,128]{3,0,2,1:T(8,128)S(1)} %copy.37, f32[5,5,48,1,1,1]{2,0,1,5,4,3:T(8,128)S(1)} %convolution_bitcast_fusion.96), kind=kOutput, calls=%fused_computation.4 | convolution fusion | flops 355000320 | bytes 5378752 | tf_op jit(solution)/shard_map/cdr,raxyz->cdaxyz/dot_general | solution.py:132
  409.0 3.8 collective-permute-start.16
  412.8 2.3 collective-permute-start.17
  416.8 4.4 collective-permute-done.17
  459.9 2.6 fusion.180
  (364 shorter events, 181.7 us)
Async XLA Ops:
  6.5 12.0 %copy-start = (f32[27,3,3]{0,2,1:T(4,128)S(1)}, f32[27,3,3]{0,2,1:T(4,128)}, u32[]{:S(2)}) copy-start(f32[27,3,3]{0,2,1:T(4,128)} %param.7) | copy-start | bytes 2920
  6.5 89.7 %all-gather.5.cloned.1.call-start = ((), (), s32[]{:S(2)}) async-start(), calls=%async_computation | async-start | bytes 1671168 | tf_op jit(solution)/shard_map/all_gather | solution.py:128
  11.6 7.2 %collective-permute-start = (f32[1,3,1,32,128]{4,1,3,2,0:T(4,128)S(1)}, f32[1,3,1,32,128]{4,1,3,2,0:T(4,128)S(1)}, u32[]{:S(2)}, u32[]{:S(2)}) collective-permute-start(f32[1,3,1,32,128]{4,1,3,2,0:T(4,128)S(1)} %get-tuple-element.126), channel_id=1, source_target_pairs={{0,16},{16,32},{32,48},{48,64},{64,80},{80,96},{96,112},{1,17},{17... | collective-permute-start | bytes 147464 | tf_op jit(solution)/shard_map/ppermute | solution.py:22
  16.2 5.6 %collective-permute-start.1 = (f32[1,3,1,32,128]{4,1,3,2,0:T(4,128)S(1)}, f32[1,3,1,32,128]{4,1,3,2,0:T(4,128)S(1)}, u32[]{:S(2)}, u32[]{:S(2)}) collective-permute-start(f32[1,3,1,32,128]{4,1,3,2,0:T(4,128)S(1)} %get-tuple-element.127), channel_id=1, source_target_pairs={{16,0},{32,16},{48,32},{64,48},{80,64},{96,80},{112,96},{17,1},{33... | collective-permute-start | bytes 147464 | tf_op jit(solution)/shard_map/ppermute | solution.py:24
  32.8 4.9 %collective-permute-start.2 = (f32[1,3,1,32,128]{4,1,3,2,0:T(4,128)S(1)}, f32[1,3,1,32,128]{4,1,3,2,0:T(4,128)S(1)}, u32[]{:S(2)}, u32[]{:S(2)}) collective-permute-start(f32[1,3,1,32,128]{4,1,3,2,0:T(4,128)S(1)} %get-tuple-element.124), channel_id=1, source_target_pairs={{0,16},{16,32},{32,48},{48,64},{64,80},{80,96},{96,112},{1,17},{17... | collective-permute-start | bytes 147464 | tf_op jit(solution)/shard_map/ppermute | solution.py:22
  34.8 5.6 %collective-permute-start.3 = (f32[1,3,1,32,128]{4,1,3,2,0:T(4,128)S(1)}, f32[1,3,1,32,128]{4,1,3,2,0:T(4,128)S(1)}, u32[]{:S(2)}, u32[]{:S(2)}) collective-permute-start(f32[1,3,1,32,128]{4,1,3,2,0:T(4,128)S(1)} %get-tuple-element.125), channel_id=1, source_target_pairs={{16,0},{32,16},{48,32},{64,48},{80,64},{96,80},{112,96},{17,1},{33... | collective-permute-start | bytes 147464 | tf_op jit(solution)/shard_map/ppermute | solution.py:24
  50.4 1.6 copy-start.3
  50.4 1.7 copy-start.2
  50.8 2.3 copy-start.4
  50.9 2.3 copy-start.5
  52.0 129.7 %all-gather.7.cloned.1.call-start = ((), (), s32[]{:S(2)}) async-start(), calls=%async_computation.1 | async-start | bytes 1671168 | tf_op jit(solution)/shard_map/all_gather | solution.py:128
  99.7 7.6 %collective-permute-start.4 = (f32[1,3,1,32,128]{4,1,3,2,0:T(4,128)S(1)}, f32[1,3,1,32,128]{4,1,3,2,0:T(4,128)S(1)}, u32[]{:S(2)}, u32[]{:S(2)}) collective-permute-start(f32[1,3,1,32,128]{4,1,3,2,0:T(4,128)S(1)} %get-tuple-element.122), channel_id=1, source_target_pairs={{0,16},{16,32},{32,48},{48,64},{64,80},{80,96},{96,112},{1,17},{17... | collective-permute-start | bytes 147464 | tf_op jit(solution)/shard_map/ppermute | solution.py:22
  104.7 5.6 %collective-permute-start.5 = (f32[1,3,1,32,128]{4,1,3,2,0:T(4,128)S(1)}, f32[1,3,1,32,128]{4,1,3,2,0:T(4,128)S(1)}, u32[]{:S(2)}, u32[]{:S(2)}) collective-permute-start(f32[1,3,1,32,128]{4,1,3,2,0:T(4,128)S(1)} %get-tuple-element.123), channel_id=1, source_target_pairs={{16,0},{32,16},{48,32},{64,48},{80,64},{96,80},{112,96},{17,1},{33... | collective-permute-start | bytes 147464 | tf_op jit(solution)/shard_map/ppermute | solution.py:24
  121.4 4.9 %collective-permute-start.6 = (f32[1,3,1,32,128]{4,1,3,2,0:T(4,128)S(1)}, f32[1,3,1,32,128]{4,1,3,2,0:T(4,128)S(1)}, u32[]{:S(2)}, u32[]{:S(2)}) collective-permute-start(f32[1,3,1,32,128]{4,1,3,2,0:T(4,128)S(1)} %get-tuple-element.120), channel_id=1, source_target_pairs={{0,16},{16,32},{32,48},{48,64},{64,80},{80,96},{96,112},{1,17},{17... | collective-permute-start | bytes 147464 | tf_op jit(solution)/shard_map/ppermute | solution.py:22
  123.4 5.6 %collective-permute-start.7 = (f32[1,3,1,32,128]{4,1,3,2,0:T(4,128)S(1)}, f32[1,3,1,32,128]{4,1,3,2,0:T(4,128)S(1)}, u32[]{:S(2)}, u32[]{:S(2)}) collective-permute-start(f32[1,3,1,32,128]{4,1,3,2,0:T(4,128)S(1)} %get-tuple-element.121), channel_id=1, source_target_pairs={{16,0},{32,16},{48,32},{64,48},{80,64},{96,80},{112,96},{17,1},{33... | collective-permute-start | bytes 147464 | tf_op jit(solution)/shard_map/ppermute | solution.py:24
  140.6 126.6 %all-gather.9.cloned.1.call-start = ((), (), s32[]{:S(2)}) async-start(), calls=%async_computation.2 | async-start | bytes 1671168 | tf_op jit(solution)/shard_map/all_gather | solution.py:128
  185.2 7.6 %collective-permute-start.8 = (f32[1,3,1,32,128]{4,1,3,2,0:T(4,128)S(1)}, f32[1,3,1,32,128]{4,1,3,2,0:T(4,128)S(1)}, u32[]{:S(2)}, u32[]{:S(2)}) collective-permute-start(f32[1,3,1,32,128]{4,1,3,2,0:T(4,128)S(1)} %get-tuple-element.118), channel_id=1, source_target_pairs={{0,16},{16,32},{32,48},{48,64},{64,80},{80,96},{96,112},{1,17},{17... | collective-permute-start | bytes 147464 | tf_op jit(solution)/shard_map/ppermute | solution.py:22
  190.1 5.6 %collective-permute-start.9 = (f32[1,3,1,32,128]{4,1,3,2,0:T(4,128)S(1)}, f32[1,3,1,32,128]{4,1,3,2,0:T(4,128)S(1)}, u32[]{:S(2)}, u32[]{:S(2)}) collective-permute-start(f32[1,3,1,32,128]{4,1,3,2,0:T(4,128)S(1)} %get-tuple-element.119), channel_id=1, source_target_pairs={{16,0},{32,16},{48,32},{64,48},{80,64},{96,80},{112,96},{17,1},{33... | collective-permute-start | bytes 147464 | tf_op jit(solution)/shard_map/ppermute | solution.py:24
  206.9 4.9 %collective-permute-start.10 = (f32[1,3,1,32,128]{4,1,3,2,0:T(4,128)S(1)}, f32[1,3,1,32,128]{4,1,3,2,0:T(4,128)S(1)}, u32[]{:S(2)}, u32[]{:S(2)}) collective-permute-start(f32[1,3,1,32,128]{4,1,3,2,0:T(4,128)S(1)} %get-tuple-element.116), channel_id=1, source_target_pairs={{0,16},{16,32},{32,48},{48,64},{64,80},{80,96},{96,112},{1,17},{17... | collective-permute-start | bytes 147464 | tf_op jit(solution)/shard_map/ppermute | solution.py:22
  208.8 5.6 %collective-permute-start.11 = (f32[1,3,1,32,128]{4,1,3,2,0:T(4,128)S(1)}, f32[1,3,1,32,128]{4,1,3,2,0:T(4,128)S(1)}, u32[]{:S(2)}, u32[]{:S(2)}) collective-permute-start(f32[1,3,1,32,128]{4,1,3,2,0:T(4,128)S(1)} %get-tuple-element.117), channel_id=1, source_target_pairs={{16,0},{32,16},{48,32},{64,48},{80,64},{96,80},{112,96},{17,1},{33... | collective-permute-start | bytes 147464 | tf_op jit(solution)/shard_map/ppermute | solution.py:24
  224.5 1.7 copy-start.1
  226.1 171.7 %all-gather.11.cloned.1.call-start = ((), (), s32[]{:S(2)}) async-start(), calls=%async_computation.3 | async-start | bytes 5013504 | tf_op jit(solution)/shard_map/all_gather | solution.py:128
  272.6 8.1 %collective-permute-start.12 = (f32[3,3,1,32,128]{4,1,3,2,0:T(4,128)S(1)}, f32[3,3,1,32,128]{4,1,3,2,0:T(4,128)S(1)}, u32[]{:S(2)}, u32[]{:S(2)}) collective-permute-start(f32[3,3,1,32,128]{4,1,3,2,0:T(4,128)S(1)} %get-tuple-element.66), channel_id=1, source_target_pairs={{0,16},{16,32},{32,48},{48,64},{64,80},{80,96},{96,112},{1,17},{17... | collective-permute-start | bytes 442376 | tf_op jit(solution)/shard_map/ppermute | solution.py:22
  277.5 7.0 %collective-permute-start.13 = (f32[3,3,1,32,128]{4,1,3,2,0:T(4,128)S(1)}, f32[3,3,1,32,128]{4,1,3,2,0:T(4,128)S(1)}, u32[]{:S(2)}, u32[]{:S(2)}) collective-permute-start(f32[3,3,1,32,128]{4,1,3,2,0:T(4,128)S(1)} %get-tuple-element.67), channel_id=1, source_target_pairs={{16,0},{32,16},{48,32},{64,48},{80,64},{96,80},{112,96},{17,1},{33... | collective-permute-start | bytes 442376 | tf_op jit(solution)/shard_map/ppermute | solution.py:24
  310.5 5.1 %collective-permute-start.14 = (f32[3,3,1,32,128]{4,1,3,2,0:T(4,128)S(1)}, f32[3,3,1,32,128]{4,1,3,2,0:T(4,128)S(1)}, u32[]{:S(2)}, u32[]{:S(2)}) collective-permute-start(f32[3,3,1,32,128]{4,1,3,2,0:T(4,128)S(1)} %get-tuple-element.64), channel_id=1, source_target_pairs={{0,16},{16,32},{32,48},{48,64},{64,80},{80,96},{96,112},{1,17},{17... | collective-permute-start | bytes 442376 | tf_op jit(solution)/shard_map/ppermute | solution.py:22
  312.5 7.0 %collective-permute-start.15 = (f32[3,3,1,32,128]{4,1,3,2,0:T(4,128)S(1)}, f32[3,3,1,32,128]{4,1,3,2,0:T(4,128)S(1)}, u32[]{:S(2)}, u32[]{:S(2)}) collective-permute-start(f32[3,3,1,32,128]{4,1,3,2,0:T(4,128)S(1)} %get-tuple-element.65), channel_id=1, source_target_pairs={{16,0},{32,16},{48,32},{64,48},{80,64},{96,80},{112,96},{17,1},{33... | collective-permute-start | bytes 442376 | tf_op jit(solution)/shard_map/ppermute | solution.py:24
  409.0 7.8 %collective-permute-start.16 = (f32[5,3,1,32,128]{4,1,3,2,0:T(4,128)S(1)}, f32[5,3,1,32,128]{4,1,3,2,0:T(4,128)S(1)}, u32[]{:S(2)}, u32[]{:S(2)}) collective-permute-start(f32[5,3,1,32,128]{4,1,3,2,0:T(4,128)S(1)} %get-tuple-element.62), channel_id=1, source_target_pairs={{0,16},{16,32},{32,48},{48,64},{64,80},{80,96},{96,112},{1,17},{17... | collective-permute-start | bytes 737288 | tf_op jit(solution)/shard_map/ppermute | solution.py:22
  412.8 8.4 %collective-permute-start.17 = (f32[5,3,1,32,128]{4,1,3,2,0:T(4,128)S(1)}, f32[5,3,1,32,128]{4,1,3,2,0:T(4,128)S(1)}, u32[]{:S(2)}, u32[]{:S(2)}) collective-permute-start(f32[5,3,1,32,128]{4,1,3,2,0:T(4,128)S(1)} %get-tuple-element.63), channel_id=1, source_target_pairs={{16,0},{32,16},{48,32},{64,48},{80,64},{96,80},{112,96},{17,1},{33... | collective-permute-start | bytes 737288 | tf_op jit(solution)/shard_map/ppermute | solution.py:24
Sparse Core Ops, SparseCore 0:
  52.1 44.0 all-gather.4
  140.7 40.9 all-gather.6
  226.2 40.9 all-gather.8
  345.5 52.1 all-gather.10
where the time goes:
time: 479 us; the launch traced here: 471 us
  waiting for transfers between devices  202 us (42%)
  matrix products  175 us (37%)
  starting transfers between devices  52.5 us (11%)
  local copies, waits for them, and re-layouts  20.4 us (4%)
  between operations  17.9 us (4%)
    all_gather x4, waiting for transfers between devices, on_device(): piece = lax.all_gather(prev_image, 'terms', axis=0, tiled=True)  173 us
    dot_general x243, matrix products, apply_stencil(): jnp.einsum('ab,sbxyz->saxyz', block_coef, window, precision=lax.Precision...  149 us
    ppermute x9, starting transfers between devices, with_halo(): lax.ppermute(tail, axis, [(i, (i + 1) % count) for i in range(ends)])  30.9 us
    ppermute x9, waiting for transfers between devices, with_halo(): lax.ppermute(head, axis, [((i + 1) % count, i) for i in range(ends)])  28.7 us
    dot_general x4, matrix products, on_device(): jnp.einsum('cdr,raxyz->cdaxyz', jnp.einsum('ct,tdq,rq->cdr', child_hot, l...  21.9 us
    ppermute x9, starting transfers between devices, with_halo(): lax.ppermute(head, axis, [((i + 1) % count, i) for i in range(ends)])  21.4 us
    slice x30, local copies, waits for them, and re-layouts, shifted(): lax.slice_in_dim(array, 0, length - 1, axis=axis_dim)  9.85 us
  transfers between devices with their start and end apart: 22, of which 14 were waited for; matrix products, arithmetic and copies ran while one was open for 2% of the time, Pallas kernels for 0%

commit v1 on v0

v1 whole, which is shorter than its diff:
```python
import functools

import jax
import jax.numpy as jnp
import numpy as np
from jax import lax
from jax.experimental import pallas as pl
from jax.experimental.pallas import tpu as pltpu
from jax.sharding import PartitionSpec as P

DIMS = 5
DEGREE = 4
TERMS = 126
GROUPS = 16
SLOT_DEV = 11
COUNT = (1, 5, 15, 35, 70)
START = (0, 1, 6, 21, 56)
CAP = (1, 1, 1, 3, 5)
BASE = (0, 1, 2, 3, 6)
T8 = (8, 8, 16, 40, 72)
T16 = (16, 16, 16, 48, 80)
WIDE = (True, True, True, False, False)
CHUNKS = ((0, 3, 20, 40), (3, 3, 20, 40), (6, 5, 32, 64))
CHUNK_OF = ((0, 0), (0, 1), (0, 2), (1, 0), (2, 0))
DIRS = tuple((dx, dy) for dx in (-1, 0, 1) for dy in (-1, 0, 1) if (dx, dy) != (0, 0))


def compositions(total, pieces_left):
    if pieces_left == 1:
        return [[total]]
    result = []
    for leading in range(total, -1, -1):
        for remainder in compositions(total - leading, pieces_left - 1):
            result.append([leading] + remainder)
    return result


def parent_hot(level):
    below = {tuple(v): n for n, v in enumerate(compositions(level - 1, DIMS))}
    hot = np.zeros((DIMS, T16[level], T16[level - 1]), np.float32)
    for n, v in enumerate(compositions(level, DIMS)):
        for d in range(DIMS):
            if v[d] > 0:
                w = list(v)
                w[d] -= 1
                hot[d, n, below[tuple(w)]] = 1.0
    hot = hot.reshape(DIMS * T16[level], T16[level - 1])
    return np.concatenate([hot, hot, hot], axis=1)


def parts3(x):
    hi = x.astype(jnp.bfloat16)
    rest = x - hi.astype(jnp.float32)
    mid = rest.astype(jnp.bfloat16)
    lo = (rest - mid.astype(jnp.float32)).astype(jnp.bfloat16)
    return hi, mid, lo


def dot(a, b):
    return jnp.dot(a, b, preferred_element_type=jnp.float32)


def dot3(hot, x):
    hi, mid, lo = parts3(x)
    return dot(hot, hi) + dot(hot, mid) + dot(hot, lo)


def term_of(i):
    q, r = i // 4, i % 4
    return q * 4 + r + (q % 2) * (3 - 2 * r)


def kernel(ns, fin, fl, cp, a1, a2, a3, a4, slots, sten, out, *scr):
    it = iter(scr)
    sb = [next(it) for _ in range(3)]
    rb = [next(it) for _ in range(3)]
    ob = [next(it) for _ in range(3)]
    qb = [next(it) for _ in range(3)]
    load_buf = [next(it) for _ in range(5)]
    sett_buf = [next(it) for _ in range(5)]
    img_buf = [next(it) for _ in range(4)]
    ct = next(it)
    ff = next(it)
    cps = next(it)
    st = next(it)
    in_s, in_r, out_s, out_r, h_s, h_r = [next(it) for _ in range(6)]
    hots = (None, a1, a2, a3, a4)

    s = lax.axis_index("space")
    k = lax.axis_index("terms")
    i = term_of(k)

    barrier = pltpu.get_barrier_semaphore()

    def greet(p, _):
        pl.semaphore_signal(
            barrier, inc=1, device_id={"terms": term_of((i + p) % GROUPS)},
            device_id_type=pl.DeviceIdType.MESH,
        )
        return 0

    lax.fori_loop(1, GROUPS, greet, 0)
    for dx, dy in DIRS:
        if dx == 0:
            continue
        there = (s + dx >= 0) & (s + dx < ns) & (i + dy >= 0) & (i + dy < GROUPS)

        @pl.when(there)
        def _():
            pl.semaphore_signal(
                barrier, inc=1,
                device_id={"space": s + dx, "terms": term_of(i + dy)},
                device_id_type=pl.DeviceIdType.MESH,
            )

    for c, (j0, n, ry, rd) in enumerate(CHUNKS):
        def pack(t, _, c=c, j0=j0, n=n, ry=ry):
            j, cx = t // 6, t % 6
            for q in range(4):
                v = fin[pl.ds(pl.multiple_of((j0 * 6 + t) * 32 + 8 * q, 8), 8), :]
                sb[c][pl.ds(8 * q * ry + cx * n + j, 8, stride=ry), :] = v
            return 0

        lax.fori_loop(0, n * 6, pack, 0)

    sides = jnp.where((s > 0) & (s < ns - 1), 2, 1) if ns > 1 else 0
    rows_of = jnp.where((i > 0) & (i < GROUPS - 1), 3, 2)
    pl.semaphore_wait(barrier, GROUPS - 1 + sides * rows_of)

    def transpose_copy(c, p, src, dst, s_sem, r_sem, rd, inward):
        i2 = (i + p) % GROUPS
        k2 = term_of(i2)
        a = i2 if inward else k2
        b = k if inward else i
        return pltpu.make_async_remote_copy(
            src_ref=src.at[pl.ds(pl.multiple_of(a * rd, 8), rd), :],
            dst_ref=dst.at[pl.ds(pl.multiple_of(b * rd, 8), rd), :],
            send_sem=s_sem.at[c, p],
            recv_sem=r_sem.at[c, p],
            device_id={"terms": k2},
            device_id_type=pl.DeviceIdType.MESH,
        )

    def arrival(c, p, src, dst, s_sem, r_sem, rd, inward):
        i2 = (i - p + GROUPS) % GROUPS
        k2 = term_of(i2)
        b = k2 if inward else i2
        return pltpu.make_async_remote_copy(
            src_ref=src.at[pl.ds(0, rd), :],
            dst_ref=dst.at[pl.ds(pl.multiple_of(b * rd, 8), rd), :],
            send_sem=s_sem.at[c, p],
            recv_sem=r_sem.at[c, p],
            device_id={"terms": k2},
            device_id_type=pl.DeviceIdType.MESH,
        )

    def send_all(c, src, dst, s_sem, r_sem, rd, inward):
        def one(p, _):
            transpose_copy(c, p, src, dst, s_sem, r_sem, rd, inward).start()
            return 0

        lax.fori_loop(1, GROUPS, one, 0)
        a = i if inward else k
        b = k if inward else i
        dst[pl.ds(pl.multiple_of(b * rd, 8), rd), :] = src[pl.ds(pl.multiple_of(a * rd, 8), rd), :]

    def wait_all(c, src, dst, s_sem, r_sem, rd, inward):
        def one(p, _):
            arrival(c, p, src, dst, s_sem, r_sem, rd, inward).wait_recv()
            return 0

        lax.fori_loop(1, GROUPS, one, 0)

    def sent_all(c, src, dst, s_sem, r_sem, rd, inward):
        def one(p, _):
            transpose_copy(c, p, src, dst, s_sem, r_sem, rd, inward).wait_send()
            return 0

        lax.fori_loop(1, GROUPS, one, 0)

    for c in range(3):
        send_all(c, sb[c], rb[c], in_s, in_r, CHUNKS[c][3], True)

    inv = [1.0 / jnp.full((8, 128), sten[13, a, a], jnp.float32) for a in range(3)]

    def table(o, _):
        for a in range(3):
            for b in range(3):
                v = jnp.full((8, 128), sten[o, a, b], jnp.float32)
                ct[1, o * 9 + a * 3 + b] = v
                ct[0, o * 9 + a * 3 + b] = -(v * inv[a]) * inv[b]
        return 0

    lax.fori_loop(0, 27, table, 0)
    for a in range(3):
        ct[0, 13 * 9 + a * 4] = inv[a]
    cps[...] = jnp.zeros_like(cps)
    cps[0:TERMS, :] = cp[...]
    for d in range(DIMS):
        for x in range(2):
            for y in range(2):
                ff[d, x, y] = jnp.broadcast_to(fl[d, x, pl.ds(2 * i + y, 1), :], (8, 128))
    for lv in range(5):
        st[lv] = jnp.full((128, 128), -1, jnp.int32)
        for j in range(CAP[lv]):
            for g in range(GROUPS):
                st[lv, j * GROUPS + g : j * GROUPS + g + 1, :] = jnp.full(
                    (1, 128), slots[g * SLOT_DEV + BASE[lv] + j], jnp.int32
                )

    def zero_outside(buf, o):
        n = 2 * o + 2
        rows = buf.shape[3]

        def clear(x0, x1, y0, y1):
            def one(c, _):
                for x in range(x0, x1):
                    for y in range(y0, y1):
                        buf[c, x, y] = jnp.zeros((rows, 128), jnp.float32)
                return 0

            lax.fori_loop(0, 3, one, 0)

        pl.when(s == 0)(lambda: clear(0, o, 0, n))
        pl.when(s == ns - 1)(lambda: clear(o + 2, n, 0, n))
        pl.when(i == 0)(lambda: clear(0, n, 0, o))
        pl.when(i == GROUPS - 1)(lambda: clear(0, n, o + 2, n))

    for lv in range(5):
        zero_outside(load_buf[lv], 2 if WIDE[lv] else 1)
        if lv < 4 and not WIDE[lv]:
            zero_outside(sett_buf[lv], 1)
        if T8[lv] < T16[lv]:
            pad = jnp.zeros((T16[lv] - T8[lv], 128), jnp.float32)
            for c in range(3):
                for x in range(2):
                    for y in range(2):
                        sett_buf[lv][c, 1 + x, 1 + y, T8[lv] :, :] = pad
                        if lv < 4:
                            img_buf[lv][2 * c + x, y, T8[lv] :, :] = pad

    lane = lax.broadcasted_iota(jnp.int32, (8, 128), 1)

    def stencil(src, bx, by, row, which):
        acc = [[[None] * 3 for _ in range(4)] for _ in range(3)]
        for dx in range(3):
            for dy in range(3):
                for b in range(3):
                    coef = [
                        [ct[which, (dx * 9 + dy * 3 + dz) * 9 + a * 3 + b] for dz in range(3)]
                        for a in range(3)
                    ]
                    for p in range(4):
                        v = src[b, bx + p // 2 + dx, by + p % 2 + dy, pl.ds(row, 8), :]
                        for a in range(3):
                            for dz in range(3):
                                t = coef[a][dz] * v
                                old = acc[a][p][dz]
                                acc[a][p][dz] = t if old is None else old + t
        res = []
        for a in range(3):
            line = []
            for p in range(4):
                low, mid, high = acc[a][p]
                low = jnp.where(lane > 0, pltpu.roll(low, 1, 1), 0.0)
                high = jnp.where(lane < 127, pltpu.roll(high, 127, 1), 0.0)
                line.append(mid + low + high)
            res.append(line)
        return res

    def halo_copy(e, n, buf, o, wide):
        dx, dy = DIRS[n]
        w = 2 if wide else 1
        rng = {1: (o + 2 - w, o - w, w), -1: (o, o + 2, w), 0: (o, o, 2)}
        sx, tx, wx = rng[dx]
        sy, ty, wy = rng[dy]
        return pltpu.make_async_remote_copy(
            src_ref=buf.at[:, sx : sx + wx, sy : sy + wy],
            dst_ref=buf.at[:, tx : tx + wx, ty : ty + wy],
            send_sem=h_s.at[e, n],
            recv_sem=h_r.at[e, n],
            device_id={"space": s + dx, "terms": term_of(i + dy)},
            device_id_type=pl.DeviceIdType.MESH,
        )

    def inside(dx, dy):
        return (s + dx >= 0) & (s + dx < ns) & (i + dy >= 0) & (i + dy < GROUPS)

    def halo_start(e, buf, o, wide):
        for n, (dx, dy) in enumerate(DIRS):
            pl.when(inside(dx, dy))(lambda n=n: halo_copy(e, n, buf, o, wide).start())

    def halo_wait(e, buf, o, wide):
        for n, (dx, dy) in enumerate(DIRS):
            pl.when(inside(-dx, -dy))(lambda n=n: halo_copy(e, n, buf, o, wide).wait_recv())

    def halo_sent(e, buf, o, wide):
        for n, (dx, dy) in enumerate(DIRS):
            pl.when(inside(dx, dy))(lambda n=n: halo_copy(e, n, buf, o, wide).wait_send())

    exchanges = []

    def exchange(buf, o, wide):
        e = len(exchanges)
        exchanges.append((e, buf, o, wide))
        halo_start(e, buf, o, wide)
        halo_wait(e, buf, o, wide)

    for lv in range(5):
        c, j0 = CHUNK_OF[lv]
        _, n, ry, rd = CHUNKS[c]
        t8, t16 = T8[lv], T16[lv]
        o = 2 if WIDE[lv] else 1
        if lv == 0 or c != CHUNK_OF[lv - 1][0]:
            wait_all(c, sb[c], rb[c], in_s, in_r, rd, True)
        terms_row = lax.broadcasted_iota(jnp.int32, (128, 128), 1) + START[lv]
        hot = (st[lv] == terms_row).astype(jnp.float32)
        to_slot = hot[0 : 16 * CAP[lv], 0:t16].astype(jnp.bfloat16)
        to_term = jnp.transpose(hot)[0:t16, 0 : 16 * CAP[lv]].astype(jnp.bfloat16)
        if lv > 0:
            weight = [
                jnp.broadcast_to(cps[START[lv] : START[lv] + t16, d : d + 1], (t16, 128))
                for d in range(DIMS)
            ]

        def load_of(cx, _):
            cc, x = cx // 2, cx % 2
            given = []
            for y in range(2):
                pieces = [
                    rb[c][pl.ds(8 * h * rd + y * ry + cx * n + j0 + j, 8, stride=rd), :]
                    for j in range(CAP[lv])
                    for h in range(2)
                ]
                given.append(jnp.concatenate(pieces, axis=0))
            value = dot3(to_term, jnp.concatenate(given, axis=1))
            if lv > 0:
                below = jnp.concatenate([img_buf[lv - 1][cx, 0], img_buf[lv - 1][cx, 1]], axis=1)
                picked = dot(hots[lv][...], jnp.concatenate(parts3(below), axis=0))
            for y in range(2):
                part = value[0:t8, 128 * y : 128 * y + 128]
                if lv > 0:
                    for d in range(DIMS):
                        field = ff[d, x, y, 0:1, :]
                        term = picked[d * t16 : d * t16 + t8, 128 * y : 128 * y + 128]
                        part = part - (weight[d][0:t8] * field) * term
                load_buf[lv][cc, o + x, o + y] = part
            return 0

        lax.fori_loop(0, 6, load_of, 0)
        exchange(load_buf[lv], o, WIDE[lv])

        if WIDE[lv]:
            def settle(t, _):
                r, q = t // 4, t % 4
                qx, qy = q // 2, q % 2
                row = pl.multiple_of(r * 8, 8)
                res = stencil(load_buf[lv], 2 * qx, 2 * qy, row, 0)
                mx = [
                    jnp.where((qx == 0) & (s == 0), 0.0, 1.0),
                    jnp.where((qx == 1) & (s == ns - 1), 0.0, 1.0),
                ]
                my = [
                    jnp.where((qy == 0) & (i == 0), 0.0, 1.0),
                    jnp.where((qy == 1) & (i == GROUPS - 1), 0.0, 1.0),
                ]
                for a in range(3):
                    for p in range(4):
                        keep = mx[p // 2] * my[p % 2]
                        sett_buf[lv][a, 2 * qx + p // 2, 2 * qy + p % 2, pl.ds(row, 8), :] = (
                            res[a][p] * keep
                        )
                return 0

            lax.fori_loop(0, t8 // 8 * 4, settle, 0)
        else:
            def settle(t, _):
                row = pl.multiple_of(t * 8, 8)
                res = stencil(load_buf[lv], 0, 0, row, 0)
                for a in range(3):
                    for p in range(4):
                        sett_buf[lv][a, 1 + p // 2, 1 + p % 2, pl.ds(row, 8), :] = res[a][p]
                return 0

            lax.fori_loop(0, t8 // 8, settle, 0)
            if lv < 4:
                exchange(sett_buf[lv], 1, False)

        if lv < 4:
            def image(t, _):
                row = pl.multiple_of(t * 8, 8)
                res = stencil(sett_buf[lv], 0, 0, row, 1)
                for a in range(3):
                    for p in range(4):
                        img_buf[lv][2 * a + p // 2, p % 2, pl.ds(row, 8), :] = res[a][p]
                return 0

            lax.fori_loop(0, t8 // 8, image, 0)

        def deliver(cx, _):
            cc, x = cx // 2, cx % 2
            both = jnp.concatenate(
                [sett_buf[lv][cc, 1 + x, 1], sett_buf[lv][cc, 1 + x, 2]], axis=1
            )
            rows = dot3(to_slot, both)
            for y in range(2):
                for j in range(CAP[lv]):
                    for h in range(2):
                        q = j * 16 + h * 8
                        ob[c][pl.ds(8 * h * rd + y * ry + cx * n + j0 + j, 8, stride=rd), :] = (
                            rows[q : q + 8, 128 * y : 128 * y + 128]
                        )
            return 0

        lax.fori_loop(0, 6, deliver, 0)
        if lv == 4 or CHUNK_OF[lv + 1][0] != c:
            send_all(c, ob[c], qb[c], out_s, out_r, rd, False)

    for c, (j0, n, ry, rd) in enumerate(CHUNKS):
        wait_all(c, ob[c], qb[c], out_s, out_r, rd, False)

        def unpack(t, _, c=c, j0=j0, n=n, ry=ry):
            j, cx = t // 6, t % 6
            for q in range(4):
                v = qb[c][pl.ds(8 * q * ry + cx * n + j, 8, stride=ry), :]
                out[pl.ds(pl.multiple_of((j0 * 6 + t) * 32 + 8 * q, 8), 8), :] = v
            return 0

        lax.fori_loop(0, n * 6, unpack, 0)

    for c in range(3):
        sent_all(c, sb[c], rb[c], in_s, in_r, CHUNKS[c][3], True)
        sent_all(c, ob[c], qb[c], out_s, out_r, CHUNKS[c][3], False)
    for args in exchanges:
        halo_sent(*args)


def on_device(ns, forcing, stencil, fields, coupling, slot_term):
    rows = forcing.shape[0] * 6 * 32
    vm = pl.BlockSpec(memory_space=pltpu.VMEM)
    sm = pl.BlockSpec(memory_space=pltpu.SMEM)
    f32 = jnp.float32
    message = lambda: [pltpu.VMEM((GROUPS * c[3], 128), f32) for c in CHUNKS]
    scratch = message() + message() + message() + message()
    for lv in range(5):
        side = 6 if WIDE[lv] else 4
        scratch.append(pltpu.VMEM((3, side, side, T8[lv], 128), f32))
    for lv in range(5):
        scratch.append(pltpu.VMEM((3, 4, 4, T16[lv], 128), f32))
    for lv in range(4):
        scratch.append(pltpu.VMEM((6, 2, T16[lv], 128), f32))
    scratch += [
        pltpu.VMEM((2, 243, 8, 128), f32),
        pltpu.VMEM((DIMS, 2, 2, 8, 128), f32),
        pltpu.VMEM((144, DIMS), f32),
        pltpu.VMEM((5, 128, 128), jnp.int32),
    ]
    dma = pltpu.SemaphoreType.DMA
    n_exchange = sum(1 if w else 2 for w in WIDE[:4]) + 1
    scratch += [dma((3, GROUPS)) for _ in range(4)] + [dma((n_exchange, 8)) for _ in range(2)]
    hots = [jnp.asarray(parent_hot(lv), jnp.bfloat16) for lv in range(1, 5)]
    out = pl.pallas_call(
        functools.partial(kernel, ns),
        out_shape=jax.ShapeDtypeStruct((rows, 128), f32),
        in_specs=[vm, vm, vm, vm, vm, vm, vm, sm, sm],
        out_specs=vm,
        scratch_shapes=scratch,
        compiler_params=pltpu.CompilerParams(
            collective_id=0, has_side_effects=True, vmem_limit_bytes=56 << 20
        ),
    )(forcing.reshape(rows, 128), fields, coupling, *hots, slot_term, stencil)
    return out.reshape(forcing.shape)


def solution(mesh):
    return jax.shard_map(
        functools.partial(on_device, mesh.shape["space"]),
        mesh=mesh,
        in_specs=(
            P("terms", None, "space", None, None),
            P(),
            P(None, "space", None, None),
            P(),
            P(),
        ),
        out_specs=P("terms", None, "space", None, None),
        check_vma=False,
    )
```

time: 479 us -> 108 us (0.23)
  the two profiles are of different devices: /device:TPU:1 before, /device:TPU:17 now
where the time goes in v1:
time: 108 us
  Pallas kernels  103 us (95%)
  local copies, waits for them, and re-layouts  5.19 us (5%)
    pallas_call x1, Pallas kernels, on_device(): pl.pallas_call(functools.partial(kernel, ns), out_shape=jax.ShapeDtypeStr...  103 us
    unnamed x3, local copies, waits for them, and re-layouts  5.19 us

profile of v1, /device:TPU:17, one launch (start us, length us, event | category | flops | bytes accessed | tf_op | source)
XLA Modules:
  0.0 107.8 jit_solution(1579406082583560902)
XLA Ops:
  0.0 1.4 %copy.11.sten = f32[27,3,3]{2,1,0:T(4,128)} copy(f32[27,3,3]{0,2,1:T(4,128)} %param.10) | data formatting | bytes 1944 | tf_op args[1]
  1.4 1.4 %copy.10.cp = f32[126,5]{1,0:T(8,128)} copy(f32[126,5]{0,1:T(8,128)} %param.12) | data formatting | bytes 5040 | tf_op args[3]
  2.9 102.6 %shard_map.91 = f32[2112,128]{1,0:T(8,128)} custom-call(f32[2112,128]{1,0:T(8,128)} %bitcast.3, f32[5,2,32,128]{3,2,1,0:T(8,128)} %fl.1, f32[126,5]{1,0:T(8,128)} %copy.10.cp, bf16[80,48]{1,0:T(8,128)(2,1)} %constant.8.clone.a1, bf16[80,48]{1,0:T(8,128)(2,1)} %constant.9.clone.a2, bf16[240,48]{1,0:T(8,128)(2,1)} %constant.10.clone.a3, ...), custom_call_target="tpu_custom_call" | custom-call | tf_op jit(solution)/shard_map/pallas_call | solution.py:462
  105.4 2.3 %copy.13 = f32[11,3,2,32,128]{4,3,2,1,0:T(8,128)} copy(f32[11,3,2,32,128]{4,3,2,1,0:T(8,128)} %bitcast.2) | data formatting | bytes 2162688

commit v2 on v0

v2 whole, which is shorter than its diff:
```python
import functools

import jax
import jax.numpy as jnp
import numpy as np
from jax import lax
from jax.experimental import pallas as pl
from jax.experimental.pallas import tpu as pltpu
from jax.sharding import PartitionSpec as P

DIMS = 5
TERMS = 126
GROUPS = 16
SLOT_DEV = 11
COUNT = (1, 5, 15, 35, 70)
START = (0, 1, 6, 21, 56)
CAP = (1, 1, 1, 3, 5)
BASE = (0, 1, 2, 3, 6)
T8 = (8, 8, 16, 40, 72)
STEP = (2, 6, 16, 12, 14)
CHUNKS = ((0, 1), (1, 2), (3, 3), (6, 5))
CHUNK_OF = ((0, 0), (1, 0), (1, 1), (2, 0), (3, 0))
DIRS = tuple((dx, dz) for dx in (-1, 0, 1) for dz in (-1, 0, 1) if (dx, dz) != (0, 0))
MESH = pl.DeviceIdType.MESH


def compositions(total, pieces_left):
    if pieces_left == 1:
        return [[total]]
    result = []
    for leading in range(total, -1, -1):
        for remainder in compositions(total - leading, pieces_left - 1):
            result.append([leading] + remainder)
    return result


def parent_table():
    table = np.full((TERMS, DIMS), -1, np.int32)
    for level in range(1, 5):
        below = {tuple(v): n for n, v in enumerate(compositions(level - 1, DIMS))}
        for n, v in enumerate(compositions(level, DIMS)):
            for d in range(DIMS):
                if v[d] > 0:
                    w = list(v)
                    w[d] -= 1
                    table[START[level] + n, d] = below[tuple(w)]
    return table.reshape(-1)


def dot(a, b):
    return jnp.dot(a, b, preferred_element_type=jnp.float32)


def term_of(i):
    q, r = i // 4, i % 4
    return q * 4 + r + (q % 2) * (3 - 2 * r)


def kernel(ns, fin, fl, cp, ptab, slots, sten, out, *scr):
    it = iter(scr)
    sb = [next(it) for _ in CHUNKS]
    rb = [next(it) for _ in CHUNKS]
    ob = [next(it) for _ in CHUNKS]
    qb = [next(it) for _ in CHUNKS]
    load_buf = [next(it) for _ in range(5)]
    sett_buf = [next(it) for _ in range(4)]
    own_buf = [next(it) for _ in range(5)]
    img_buf = [next(it) for _ in range(4)]
    faces = [next(it) for _ in range(9)]
    rims = [next(it) for _ in range(9)]
    wh, wl, xs, ff, ft, posv, pos, pos_sem = [next(it) for _ in range(8)]
    in_s, in_r, out_s, out_r, h_s, h_r = [next(it) for _ in range(6)]

    s = lax.axis_index("space")
    k = lax.axis_index("terms")
    i = term_of(k)

    barrier = pltpu.get_barrier_semaphore()

    def greet(p, _):
        pl.semaphore_signal(
            barrier, inc=1, device_id={"terms": term_of((i + p) % GROUPS)}, device_id_type=MESH
        )
        return 0

    lax.fori_loop(1, GROUPS, greet, 0)

    def inside(dx, dz):
        return (s + dx >= 0) & (s + dx < ns) & (i + dz >= 0) & (i + dz < GROUPS)

    for dx, dz in DIRS:
        if dx == 0:
            continue

        @pl.when(inside(dx, dz))
        def _():
            pl.semaphore_signal(
                barrier, inc=1,
                device_id={"space": s + dx, "terms": term_of(i + dz)},
                device_id_type=MESH,
            )

    def pack(c):
        j0, n = CHUNKS[c]

        def one(m, _):
            j, x = j0 + m // 2, m % 2
            rows = [
                fin[pl.ds(pl.multiple_of((j * 6 + a * 2 + x) * 32, 32), 32), :] for a in range(3)
            ]
            turned = jnp.transpose(jnp.concatenate(rows + [jnp.zeros((32, 128), jnp.float32)], axis=0))
            sb[c][:, m] = turned.reshape(GROUPS, 8, 128)
            return 0

        lax.fori_loop(0, 2 * n, one, 0)

    def wait_barrier():
        sides = jnp.where((s > 0) & (s < ns - 1), 2, 1) if ns > 1 else 0
        rows_of = jnp.where((i > 0) & (i < GROUPS - 1), 3, 2)
        pl.semaphore_wait(barrier, GROUPS - 1 + sides * rows_of)

    def leaving(c, p, src, dst, s_sem, r_sem, inward):
        i2 = (i + p) % GROUPS
        k2 = term_of(i2)
        return pltpu.make_async_remote_copy(
            src_ref=src.at[i2 if inward else k2],
            dst_ref=dst.at[k if inward else i],
            send_sem=s_sem.at[c, p],
            recv_sem=r_sem.at[c, p],
            device_id={"terms": k2},
            device_id_type=MESH,
        )

    def arriving(c, p, src, dst, s_sem, r_sem, inward):
        i2 = (i - p + GROUPS) % GROUPS
        k2 = term_of(i2)
        return pltpu.make_async_remote_copy(
            src_ref=src.at[0],
            dst_ref=dst.at[k2 if inward else i2],
            send_sem=s_sem.at[c, p],
            recv_sem=r_sem.at[c, p],
            device_id={"terms": k2},
            device_id_type=MESH,
        )

    def over_peers(fn):
        def one(p, _):
            fn(p)
            return 0

        lax.fori_loop(1, GROUPS, one, 0)

    def send_in(c):
        over_peers(lambda p: leaving(c, p, sb[c], rb[c], in_s, in_r, True).start())
        rb[c][k] = sb[c][i]

    def wait_in(c):
        over_peers(lambda p: arriving(c, p, sb[c], rb[c], in_s, in_r, True).wait_recv())

    def send_out(c):
        over_peers(lambda p: leaving(c, p, ob[c], qb[c], out_s, out_r, False).start())
        qb[c][i] = ob[c][k]

    def wait_out(c):
        over_peers(lambda p: arriving(c, p, ob[c], qb[c], out_s, out_r, False).wait_recv())

    pack(0)
    wait_barrier()
    send_in(0)
    pack(1)
    send_in(1)

    lane8 = lax.broadcasted_iota(jnp.int32, (8, 128), 1)

    def locate(g, acc):
        for j in range(SLOT_DEV):
            acc = jnp.where(lane8 == slots[g * SLOT_DEV + j], g * 16 + j, acc)
        return acc

    posv[...] = lax.fori_loop(0, GROUPS, locate, jnp.zeros((8, 128), jnp.int32))
    to_smem = pltpu.make_async_copy(posv, pos, pos_sem)
    to_smem.start()

    for dz in range(3):
        for which in range(2):
            for w in (wh, wl):
                w[which, (dz * 4 + 3) * 128 : (dz * 4 + 4) * 128, 0:128] = jnp.zeros(
                    (128, 128), jnp.bfloat16
                )
                w[which, dz * 512 : dz * 512 + 128, 128:256] = jnp.zeros((128, 128), jnp.bfloat16)
    lane1 = lax.broadcasted_iota(jnp.int32, (1, 128), 1)
    group = lane1 // 32

    def by_group(v0, v1, v2):
        return jnp.where(
            group == 0, v0, jnp.where(group == 1, v1, jnp.where(group == 2, v2, 0.0))
        ).astype(jnp.float32)

    def splat(v):
        return jnp.full((1, 128), v, jnp.float32)

    inv = [1.0 / splat(sten[a, a, 13]) for a in range(3)]
    inv_lane = by_group(*inv)
    apart = lax.broadcasted_iota(jnp.int32, (32, 128), 0) - lax.broadcasted_iota(
        jnp.int32, (32, 128), 1
    ) % 32

    def table(m, _):
        dx, dz = m // 3, m % 3
        for b in range(4):
            block = [jnp.zeros((32, 128), jnp.float32)] * 2
            if b < 3:
                for dy in range(3):
                    o = dx * 9 + dy * 3 + dz
                    plain = by_group(*[splat(sten[a, b, o]) for a in range(3)])
                    smooth = -(plain * inv_lane) * inv[b]
                    if dy == 1:
                        centre = (group == b) & ((dx == 1) & (dz == 1))
                        smooth = jnp.where(centre, inv_lane, smooth)
                    for which, line in enumerate((smooth, plain)):
                        block[which] = jnp.where(apart == dy - 1, line, block[which])
            for which in range(2):
                hi = block[which].astype(jnp.bfloat16)
                lo = (block[which] - hi.astype(jnp.float32)).astype(jnp.bfloat16)
                for px in range(2):
                    row = pl.multiple_of((dz * 4 + dx + px) * 128 + b * 32, 32)
                    wh[which, pl.ds(row, 32), px * 128 : px * 128 + 128] = hi
                    wl[which, pl.ds(row, 32), px * 128 : px * 128 + 128] = lo
        return 0

    lax.fori_loop(0, 9, table, 0)

    def field(m, _):
        rows = fl[m // 2, m % 2]
        ft[...] = jnp.transpose(jnp.concatenate([rows] * 4, axis=0))
        ff[m] = ft[pl.ds(pl.multiple_of(8 * i, 8), 8), :]
        return 0

    lax.fori_loop(0, 2 * DIMS, field, 0)

    def zero_outside(buf, rim, count):
        def layer(x):
            def one(t, _):
                buf[x, t] = jnp.zeros((24, 128), jnp.float32)
                return 0

            lax.fori_loop(0, count, one, 0)
            for side in range(2):
                rim[side, x] = jnp.zeros(rim.shape[2:], jnp.float32)

        pl.when(s == 0)(lambda: layer(0))
        pl.when(s == ns - 1)(lambda: layer(3))

        def edge(side):
            rim[side] = jnp.zeros(rim.shape[1:], jnp.float32)

        pl.when(i == 0)(lambda: edge(0))
        pl.when(i == GROUPS - 1)(lambda: edge(1))

    for lv in range(5):
        zero_outside(load_buf[lv], rims[2 * lv], COUNT[lv])
        if lv < 4:
            zero_outside(sett_buf[lv], rims[2 * lv + 1], COUNT[lv])

    pack(2)
    pack(3)
    to_smem.wait()

    def halo_copy(e, n, buf, count):
        dx, dz = DIRS[n]
        sx, tx = {1: (2, 0), -1: (1, 3), 0: (0, 0)}[dx]
        if dz == 0:
            src, dst = buf.at[sx, 0:count, 8:16, :], buf.at[tx, 0:count, 8:16, :]
        else:
            side = 1 if dz > 0 else 0
            if dx == 0:
                src, dst = faces[e].at[side], rims[e].at[1 - side, 1:3]
            else:
                src, dst = faces[e].at[side, sx - 1], rims[e].at[1 - side, tx]
        return pltpu.make_async_remote_copy(
            src_ref=src,
            dst_ref=dst,
            send_sem=h_s.at[e, n],
            recv_sem=h_r.at[e, n],
            device_id={"space": s + dx, "terms": term_of(i + dz)},
            device_id_type=MESH,
        )

    def by_five(count, fn):
        w = min(count, 5)

        def some(u, _):
            for v in range(w):
                fn(u * w + v)
            return 0

        lax.fori_loop(0, count // w, some, 0)

    exchanges = []

    def start_exchange(e, buf, count):
        exchanges.append((e, buf, count))
        for n, (dx, dz) in enumerate(DIRS):
            pl.when(inside(dx, dz))(lambda n=n: halo_copy(e, n, buf, count).start())

    def end_exchange(e, buf, count):
        for n, (dx, dz) in enumerate(DIRS):
            pl.when(inside(-dx, -dz))(lambda n=n: halo_copy(e, n, buf, count).wait_recv())

        def spread(t):
            for x in range(4):
                buf[x, t, 7:8, :] = rims[e][0, x, pl.ds(t, 1), :]
                buf[x, t, 16:17, :] = rims[e][1, x, pl.ds(t, 1), :]

        by_five(count, spread)

    def apply(lv, src, which, store):
        step = STEP[lv]
        rows = step * 8

        def chunk(ci, _):
            def pair(u, _):
                t = ci * step + 2 * u
                for dz in range(3):
                    for x in range(4):
                        v = jnp.concatenate(
                            [src[x, t, 7 + dz : 15 + dz, :], src[x, t + 1, 7 + dz : 15 + dz, :]], axis=0
                        )
                        hi = v.astype(jnp.bfloat16)
                        lo = (v - hi.astype(jnp.float32)).astype(jnp.bfloat16)
                        col = (dz * 4 + x) * 128
                        xs[pl.ds(pl.multiple_of(u * 16, 16), 16), col : col + 128] = hi
                        xs[pl.ds(pl.multiple_of(rows + u * 16, 16), 16), col : col + 128] = lo
                return 0

            lax.fori_loop(0, step // 2, pair, 0)
            both = dot(xs[0 : 2 * rows, :], wh[which])
            res = both[0:rows] + both[rows:] + dot(xs[0:rows, :], wl[which])
            for px in range(2):
                store(px, ci * step, res[:, px * 128 : px * 128 + 128].reshape(step, 8, 128))
            return 0

        lax.fori_loop(0, -(-COUNT[lv] // step), chunk, 0)

    e = 0
    for lv in range(5):
        c, j0 = CHUNK_OF[lv]
        step = STEP[lv]
        if lv == 0 or c != CHUNK_OF[lv - 1][0]:
            wait_in(c)
        if lv == 0:
            send_in(2)

        def load_of(t):
            q = pos[0, START[lv] + t]
            g = q // 16
            j = j0 + jnp.clip(q % 16 - BASE[lv], 0, CAP[lv] - 1)
            parts = [rb[c][g, 2 * j + x] for x in range(2)]
            if lv > 0:
                for d in range(DIMS):
                    par = ptab[(START[lv] + t) * DIMS + d]
                    weight = jnp.where(par >= 0, cp[d, START[lv] + t], 0.0)
                    at = jnp.maximum(par, 0)
                    for x in range(2):
                        parts[x] = parts[x] - (weight * ff[2 * d + x]) * img_buf[lv - 1][x, at]
            for x in range(2):
                load_buf[lv][1 + x, t, 8:16, :] = parts[x]
                faces[2 * lv][0, x, pl.ds(t, 1), :] = parts[x][0:1]
                faces[2 * lv][1, x, pl.ds(t, 1), :] = parts[x][7:8]

        by_five(COUNT[lv], load_of)
        start_exchange(2 * lv, load_buf[lv], COUNT[lv])
        end_exchange(2 * lv, load_buf[lv], COUNT[lv])
        if lv == 1:
            send_in(3)

        def settle(px, t0, v):
            own_buf[lv][px, pl.ds(t0, step)] = v
            if lv < 4:
                sett_buf[lv][1 + px, pl.ds(t0, step), 8:16, :] = v

        apply(lv, load_buf[lv], 0, settle)

        if lv < 4:
            def face(t):
                for x in range(2):
                    faces[2 * lv + 1][0, x, pl.ds(t, 1), :] = sett_buf[lv][1 + x, t, 8:9, :]
                    faces[2 * lv + 1][1, x, pl.ds(t, 1), :] = sett_buf[lv][1 + x, t, 15:16, :]

            by_five(COUNT[lv], face)
            start_exchange(2 * lv + 1, sett_buf[lv], COUNT[lv])

        def deliver(g, _):
            for j in range(CAP[lv]):
                q = slots[g * SLOT_DEV + BASE[lv] + j]
                t = jnp.clip(q - START[lv], 0, COUNT[lv] - 1)
                for x in range(2):
                    v = own_buf[lv][x, t]
                    ob[c][g, 2 * (j0 + j) + x] = jnp.where(q >= 0, v, 0.0)
            return 0

        lax.fori_loop(0, GROUPS, deliver, 0)

        if lv < 4:
            end_exchange(2 * lv + 1, sett_buf[lv], COUNT[lv])

            def image(px, t0, v):
                img_buf[lv][px, pl.ds(t0, step)] = v

            apply(lv, sett_buf[lv], 1, image)
        if lv == 4 or CHUNK_OF[lv + 1][0] != c:
            send_out(c)

    for c, (j0, n) in enumerate(CHUNKS):
        wait_out(c)

        def unpack(m, _, c=c, j0=j0):
            j, x = j0 + m // 2, m % 2
            turned = jnp.transpose(qb[c][:, m].reshape(128, 128))
            for a in range(3):
                row = pl.multiple_of((j * 6 + a * 2 + x) * 32, 32)
                out[pl.ds(row, 32), :] = turned[32 * a : 32 * a + 32]
            return 0

        lax.fori_loop(0, 2 * n, unpack, 0)

    for c in range(len(CHUNKS)):
        over_peers(lambda p: leaving(c, p, sb[c], rb[c], in_s, in_r, True).wait_send())
        over_peers(lambda p: leaving(c, p, ob[c], qb[c], out_s, out_r, False).wait_send())
    for e, buf, count in exchanges:
        for n, (dx, dz) in enumerate(DIRS):
            pl.when(inside(dx, dz))(lambda n=n: halo_copy(e, n, buf, count).wait_send())


def on_device(ns, forcing, stencil, fields, coupling, slot_term):
    rows = forcing.shape[0] * 6 * 32
    vm = pl.BlockSpec(memory_space=pltpu.VMEM)
    sm = pl.BlockSpec(memory_space=pltpu.SMEM)
    f32, bf16 = jnp.float32, jnp.bfloat16
    dma = pltpu.SemaphoreType.DMA
    scratch = [pltpu.VMEM((GROUPS, 2 * n, 8, 128), f32) for _ in range(4) for _, n in CHUNKS]
    scratch += [pltpu.VMEM((4, T8[lv], 24, 128), f32) for lv in (0, 1, 2, 3, 4, 0, 1, 2, 3)]
    scratch += [pltpu.VMEM((2, T8[lv], 8, 128), f32) for lv in range(5)]
    scratch += [pltpu.VMEM((2, T8[lv], 8, 128), f32) for lv in range(4)]
    scratch += [pltpu.VMEM((2, 2, T8[e // 2], 128), f32) for e in range(9)]
    scratch += [pltpu.VMEM((2, 4, T8[e // 2], 128), f32) for e in range(9)]
    scratch += [
        pltpu.VMEM((2, 12 * 128, 256), bf16),
        pltpu.VMEM((2, 12 * 128, 256), bf16),
        pltpu.VMEM((2 * 8 * max(STEP), 12 * 128), bf16),
        pltpu.VMEM((2 * DIMS, 8, 128), f32),
        pltpu.VMEM((128, 128), f32),
        pltpu.VMEM((8, 128), jnp.int32),
        pltpu.SMEM((8, 128), jnp.int32),
        dma(()),
    ]
    scratch += [dma((len(CHUNKS), GROUPS)) for _ in range(4)] + [dma((9, 8)) for _ in range(2)]
    out = pl.pallas_call(
        functools.partial(kernel, ns),
        out_shape=jax.ShapeDtypeStruct((rows, 128), f32),
        in_specs=[vm, vm, sm, sm, sm, sm],
        out_specs=vm,
        scratch_shapes=scratch,
        compiler_params=pltpu.CompilerParams(
            collective_id=0, has_side_effects=True, vmem_limit_bytes=56 << 20
        ),
    )(forcing.reshape(rows, 128), fields, coupling.T, jnp.asarray(parent_table()), slot_term, stencil.transpose(1, 2, 0))
    return out.reshape(forcing.shape)


def solution(mesh):
    return jax.shard_map(
        functools.partial(on_device, mesh.shape["space"]),
        mesh=mesh,
        in_specs=(
            P("terms", None, "space", None, None),
            P(),
            P(None, "space", None, None),
            P(),
            P(),
        ),
        out_specs=P("terms", None, "space", None, None),
        check_vma=False,
    )
```

time: 479 us -> 94.5 us (0.20); the launches traced: 471 us -> 92.9 us
  waiting for transfers between devices: 202 us -> 0 us
  matrix products: 175 us -> 0 us
  Pallas kernels: 0 us -> 90.5 us
  starting transfers between devices: 52.5 us -> 0 us
  local copies, waits for them, and re-layouts: 20.4 us -> 2.34 us
  between operations: 17.9 us -> 0.01 us
    dot_general x255 -> x0, matrix products: 175 us -> none  [the longest x243 149 us: apply_stencil(): jnp.einsum('ab,sbxyz->saxyz', block_coef, window, precision=lax.Precision...]
    all_gather x4 -> x0, waiting for transfers between devices: 173 us -> none  [on_device(): piece = lax.all_gather(prev_image, 'terms', axis=0, tiled=True)]
    pallas_call x0 -> x1, Pallas kernels: none -> 90.5 us  [on_device(): pl.pallas_call(functools.partial(kernel, ns), out_shape=jax.ShapeDtypeStr...]
    ppermute x18 -> x0, starting transfers between devices: 52.4 us -> none  [the longest x9 30.9 us: with_halo(): lax.ppermute(tail, axis, [(i, (i + 1) % count) for i in range(ends)])]
    ppermute x18 -> x0, waiting for transfers between devices: 29.1 us -> none  [the longest x9 28.7 us: with_halo(): lax.ppermute(head, axis, [((i + 1) % count, i) for i in range(ends)])]
    slice x54 -> x0, local copies, waits for them, and re-layouts: 14.8 us -> none  [the longest x30 9.85 us: shifted(): lax.slice_in_dim(array, 0, length - 1, axis=axis_dim)]
  transfers between devices with their start and end apart: 22 -> 0, of which waited for: 14 -> 0; matrix products, arithmetic and copies ran while one was open for 2% -> 0% of each run, Pallas kernels for 0% -> 0%
where the time goes in v2:
time: 94.5 us; the launch traced here: 92.9 us
  Pallas kernels  90.5 us (96%)
  local copies, waits for them, and re-layouts  2.34 us (2%)
    pallas_call x1, Pallas kernels, on_device(): pl.pallas_call(functools.partial(kernel, ns), out_shape=jax.ShapeDtypeStr...  90.5 us
    unnamed x1, local copies, waits for them, and re-layouts  2.34 us

profile of v2, /device:TPU:1, one launch (start us, length us, event | category | flops | bytes accessed | tf_op | source)
XLA Modules:
  0.0 92.9 jit_solution(887260967979559855)
XLA Ops:
  0.0 90.5 %shard_map.64 = f32[2112,128]{1,0:T(8,128)} custom-call(f32[2112,128]{1,0:T(8,128)} %bitcast.5, f32[5,2,32,128]{3,2,1,0:T(8,128)} %fl.1, f32[5,126]{1,0:T(8,128)} %bitcast.7, s32[630]{0:T(1024)} %constant.2.clone.ptab, s32[176]{0:T(256)} %slots.1, f32[3,3,27]{2,1,0:T(4,128)} %bitcast.6), custom_call_target="tpu_custom_call" | custom-call | tf_op jit(solution)/shard_map/pallas_call | solution.py:458
  90.6 2.3 %copy.8 = f32[11,3,2,32,128]{4,3,2,1,0:T(8,128)} copy(f32[11,3,2,32,128]{4,3,2,1,0:T(8,128)} %bitcast.4) | data formatting | bytes 2162688

commit v3 on v2

--- a/solution.py
+++ b/solution.py
@@ -17,7 +17,8 @@
 CAP = (1, 1, 1, 3, 5)
 BASE = (0, 1, 2, 3, 6)
 T8 = (8, 8, 16, 40, 72)
-STEP = (2, 6, 16, 12, 14)
+STEP = (2, 6, 16, 36, 36)
+WIDE = (True, True, True, False, False)
 CHUNKS = ((0, 1), (1, 2), (3, 3), (6, 5))
 CHUNK_OF = ((0, 0), (1, 0), (1, 1), (2, 0), (3, 0))
 DIRS = tuple((dx, dz) for dx in (-1, 0, 1) for dz in (-1, 0, 1) if (dx, dz) != (0, 0))
@@ -238,7 +239,7 @@
 
     lax.fori_loop(0, 2 * DIMS, field, 0)
 
-    def zero_outside(buf, rim, count):
+    def zero_outside(buf, rim, count, wide):
         def layer(x):
             def one(t, _):
                 buf[x, t] = jnp.zeros((24, 128), jnp.float32)
@@ -246,21 +247,30 @@
 
             lax.fori_loop(0, count, one, 0)
             for side in range(2):
-                rim[side, x] = jnp.zeros(rim.shape[2:], jnp.float32)
-
-        pl.when(s == 0)(lambda: layer(0))
-        pl.when(s == ns - 1)(lambda: layer(3))
+                if wide:
+                    for row in range(3):
+                        rim[side, row, x] = jnp.zeros(rim.shape[3:], jnp.float32)
+                else:
+                    rim[side, x] = jnp.zeros(rim.shape[2:], jnp.float32)
 
         def edge(side):
-            rim[side] = jnp.zeros(rim.shape[1:], jnp.float32)
-
+            if wide:
+                for row in (side, side + 1):
+                    rim[side, row] = jnp.zeros(rim.shape[2:], jnp.float32)
+            else:
+                rim[side] = jnp.zeros(rim.shape[1:], jnp.float32)
+
+        for x in (0, 1) if wide else (0,):
+            pl.when(s == 0)(lambda x=x: layer(x))
+        for x in (4, 5) if wide else (3,):
+            pl.when(s == ns - 1)(lambda x=x: layer(x))
         pl.when(i == 0)(lambda: edge(0))
         pl.when(i == GROUPS - 1)(lambda: edge(1))
 
     for lv in range(5):
-        zero_outside(load_buf[lv], rims[2 * lv], COUNT[lv])
-        if lv < 4:
-            zero_outside(sett_buf[lv], rims[2 * lv + 1], COUNT[lv])
+        zero_outside(load_buf[lv], rims[2 * lv], COUNT[lv], WIDE[lv])
+        if lv < 4 and not WIDE[lv]:
+            zero_outside(sett_buf[lv], rims[2 * lv + 1], COUNT[lv], False)
 
     pack(2)
     pack(3)
@@ -269,7 +279,15 @@
     def halo_copy(e, n, buf, count):
         dx, dz = DIRS[n]
         sx, tx = {1: (2, 0), -1: (1, 3), 0: (0, 0)}[dx]
-        if dz == 0:
+        if buf.shape[0] == 6:
+            tx = {1: 0, -1: 4, 0: 2}[dx]
+            if dz == 0:
+                src, dst = buf.at[2:4, 0:count, 8:16, :], buf.at[tx : tx + 2, 0:count, 8:16, :]
+            else:
+                side = 1 if dz > 0 else 0
+                src = faces[e].at[side]
+                dst = rims[e].at[1 - side, 1 - side : 3 - side, tx : tx + 2]
+        elif dz == 0:
             src, dst = buf.at[sx, 0:count, 8:16, :], buf.at[tx, 0:count, 8:16, :]
         else:
             side = 1 if dz > 0 else 0
@@ -307,12 +325,70 @@
         for n, (dx, dz) in enumerate(DIRS):
             pl.when(inside(-dx, -dz))(lambda n=n: halo_copy(e, n, buf, count).wait_recv())
 
+        spread_rim(e, buf, count)
+
+    def spread_rim(e, buf, count):
         def spread(t):
             for x in range(4):
                 buf[x, t, 7:8, :] = rims[e][0, x, pl.ds(t, 1), :]
                 buf[x, t, 16:17, :] = rims[e][1, x, pl.ds(t, 1), :]
 
-        by_five(count, spread)
+        def spread_wide(t):
+            for x in range(6):
+                buf[x, t, 7:8, :] = rims[e][0, 1, x, pl.ds(t, 1), :]
+                buf[x, t, 16:17, :] = rims[e][1, 1, x, pl.ds(t, 1), :]
+                rims[e][0, 2, x, pl.ds(t, 1), :] = buf[x, t, 8:9, :]
+                rims[e][1, 0, x, pl.ds(t, 1), :] = buf[x, t, 15:16, :]
+
+        by_five(count, spread_wide if buf.shape[0] == 6 else spread)
+
+    def halves(v):
+        hi = v.astype(jnp.bfloat16)
+        return hi, (v - hi.astype(jnp.float32)).astype(jnp.bfloat16)
+
+    def product(rows, which):
+        both = dot(xs[0 : 2 * rows, :], wh[which])
+        return both[0:rows] + both[rows:] + dot(xs[0:rows, :], wl[which])
+
+    def settle_wide(lv):
+        src, rim, step, t8 = load_buf[lv], rims[2 * lv], STEP[lv], T8[lv]
+        base = 16 * step
+        rows = base + 4 * t8
+
+        def put(row, col, v):
+            hi, lo = halves(v)
+            xs[pl.ds(pl.multiple_of(row, 16), v.shape[0]), col : col + 128] = hi
+            xs[pl.ds(pl.multiple_of(rows + row, 16), v.shape[0]), col : col + 128] = lo
+
+        def pair(u, _):
+            for dz in range(3):
+                for w in range(4):
+                    for b in range(2):
+                        v = [src[2 * b + w, 2 * u + h, 7 + dz : 15 + dz, :] for h in range(2)]
+                        put(b * 8 * step + u * 16, (dz * 4 + w) * 128, jnp.concatenate(v, axis=0))
+            return 0
+
+        lax.fori_loop(0, step // 2, pair, 0)
+        for side in range(2):
+            for dz in range(3):
+                for w in range(4):
+                    v = [rim[side, dz, 2 * b + w] for b in range(2)]
+                    put(base + side * 2 * t8, (dz * 4 + w) * 128, jnp.concatenate(v, axis=0))
+        res = product(rows, 0)
+        one, zero = jnp.float32(1.0), jnp.float32(0.0)
+        in_x = [jnp.where(s > 0, one, zero), one, one, jnp.where(s < ns - 1, one, zero)]
+        in_z = [jnp.where(i > 0, one, zero), jnp.where(i < GROUPS - 1, one, zero)]
+        for x in range(4):
+            b, lanes = x // 2, slice(128 * (x % 2), 128 * (x % 2) + 128)
+            v = res[b * 8 * step : (b + 1) * 8 * step, lanes].reshape(step, 8, 128)
+            if x in (1, 2):
+                own_buf[lv][x - 1, 0:step] = v
+            else:
+                v = v * in_x[x]
+            sett_buf[lv][x, 0:step, 8:16, :] = v
+            for side in range(2):
+                row = base + side * 2 * t8 + b * t8
+                rims[2 * lv + 1][side, x] = res[row : row + t8, lanes] * (in_x[x] * in_z[side])
 
     def apply(lv, src, which, store):
         step = STEP[lv]
@@ -326,23 +402,21 @@
                         v = jnp.concatenate(
                             [src[x, t, 7 + dz : 15 + dz, :], src[x, t + 1, 7 + dz : 15 + dz, :]], axis=0
                         )
-                        hi = v.astype(jnp.bfloat16)
-                        lo = (v - hi.astype(jnp.float32)).astype(jnp.bfloat16)
+                        hi, lo = halves(v)
                         col = (dz * 4 + x) * 128
                         xs[pl.ds(pl.multiple_of(u * 16, 16), 16), col : col + 128] = hi
                         xs[pl.ds(pl.multiple_of(rows + u * 16, 16), 16), col : col + 128] = lo
                 return 0
 
             lax.fori_loop(0, step // 2, pair, 0)
-            both = dot(xs[0 : 2 * rows, :], wh[which])
-            res = both[0:rows] + both[rows:] + dot(xs[0:rows, :], wl[which])
+            res = product(rows, which)
             for px in range(2):
                 store(px, ci * step, res[:, px * 128 : px * 128 + 128].reshape(step, 8, 128))
             return 0
 
         lax.fori_loop(0, -(-COUNT[lv] // step), chunk, 0)
 
-    e = 0
+    pending = []
     for lv in range(5):
         c, j0 = CHUNK_OF[lv]
         step = STEP[lv]
@@ -364,12 +438,19 @@
                     for x in range(2):
                         parts[x] = parts[x] - (weight * ff[2 * d + x]) * img_buf[lv - 1][x, at]
             for x in range(2):
-                load_buf[lv][1 + x, t, 8:16, :] = parts[x]
-                faces[2 * lv][0, x, pl.ds(t, 1), :] = parts[x][0:1]
-                faces[2 * lv][1, x, pl.ds(t, 1), :] = parts[x][7:8]
+                load_buf[lv][(2 if WIDE[lv] else 1) + x, t, 8:16, :] = parts[x]
+                if WIDE[lv]:
+                    for row in range(2):
+                        faces[2 * lv][0, row, x, pl.ds(t, 1), :] = parts[x][row : row + 1]
+                        faces[2 * lv][1, row, x, pl.ds(t, 1), :] = parts[x][6 + row : 7 + row]
+                else:
+                    faces[2 * lv][0, x, pl.ds(t, 1), :] = parts[x][0:1]
+                    faces[2 * lv][1, x, pl.ds(t, 1), :] = parts[x][7:8]
 
         by_five(COUNT[lv], load_of)
         start_exchange(2 * lv, load_buf[lv], COUNT[lv])
+        if pending:
+            pending.pop()()
         end_exchange(2 * lv, load_buf[lv], COUNT[lv])
         if lv == 1:
             send_in(3)
@@ -379,9 +460,13 @@
             if lv < 4:
                 sett_buf[lv][1 + px, pl.ds(t0, step), 8:16, :] = v
 
-        apply(lv, load_buf[lv], 0, settle)
-
-        if lv < 4:
+        if WIDE[lv]:
+            settle_wide(lv)
+            spread_rim(2 * lv + 1, sett_buf[lv], COUNT[lv])
+        else:
+            apply(lv, load_buf[lv], 0, settle)
+
+        if lv < 4 and not WIDE[lv]:
             def face(t):
                 for x in range(2):
                     faces[2 * lv + 1][0, x, pl.ds(t, 1), :] = sett_buf[lv][1 + x, t, 8:9, :]
@@ -390,7 +475,7 @@
             by_five(COUNT[lv], face)
             start_exchange(2 * lv + 1, sett_buf[lv], COUNT[lv])
 
-        def deliver(g, _):
+        def deliver(g, _, lv=lv, c=c, j0=j0):
             for j in range(CAP[lv]):
                 q = slots[g * SLOT_DEV + BASE[lv] + j]
                 t = jnp.clip(q - START[lv], 0, COUNT[lv] - 1)
@@ -399,17 +484,28 @@
                     ob[c][g, 2 * (j0 + j) + x] = jnp.where(q >= 0, v, 0.0)
             return 0
 
-        lax.fori_loop(0, GROUPS, deliver, 0)
+        if not WIDE[lv]:
+            lax.fori_loop(0, GROUPS, deliver, 0)
 
         if lv < 4:
-            end_exchange(2 * lv + 1, sett_buf[lv], COUNT[lv])
+            if not WIDE[lv]:
+                end_exchange(2 * lv + 1, sett_buf[lv], COUNT[lv])
 
             def image(px, t0, v):
                 img_buf[lv][px, pl.ds(t0, step)] = v
 
             apply(lv, sett_buf[lv], 1, image)
-        if lv == 4 or CHUNK_OF[lv + 1][0] != c:
-            send_out(c)
+
+        def finish(lv=lv, c=c, deliver=deliver):
+            if WIDE[lv]:
+                lax.fori_loop(0, GROUPS, deliver, 0)
+            if lv == 4 or CHUNK_OF[lv + 1][0] != c:
+                send_out(c)
+
+        if WIDE[lv]:
+            pending.append(finish)
+        else:
+            finish()
 
     for c, (j0, n) in enumerate(CHUNKS):
         wait_out(c)
@@ -439,15 +535,20 @@
     f32, bf16 = jnp.float32, jnp.bfloat16
     dma = pltpu.SemaphoreType.DMA
     scratch = [pltpu.VMEM((GROUPS, 2 * n, 8, 128), f32) for _ in range(4) for _, n in CHUNKS]
-    scratch += [pltpu.VMEM((4, T8[lv], 24, 128), f32) for lv in (0, 1, 2, 3, 4, 0, 1, 2, 3)]
+    scratch += [pltpu.VMEM((6 if WIDE[lv] else 4, T8[lv], 24, 128), f32) for lv in range(5)]
+    scratch += [pltpu.VMEM((4, T8[lv], 24, 128), f32) for lv in range(4)]
     scratch += [pltpu.VMEM((2, T8[lv], 8, 128), f32) for lv in range(5)]
     scratch += [pltpu.VMEM((2, T8[lv], 8, 128), f32) for lv in range(4)]
-    scratch += [pltpu.VMEM((2, 2, T8[e // 2], 128), f32) for e in range(9)]
-    scratch += [pltpu.VMEM((2, 4, T8[e // 2], 128), f32) for e in range(9)]
+    wide = [WIDE[e // 2] and e % 2 == 0 for e in range(9)]
+    scratch += [pltpu.VMEM((2,) + (2,) * w + (2, T8[e // 2], 128), f32) for e, w in enumerate(wide)]
+    scratch += [
+        pltpu.VMEM((2, 3, 6, T8[e // 2], 128) if w else (2, 4, T8[e // 2], 128), f32)
+        for e, w in enumerate(wide)
+    ]
     scratch += [
         pltpu.VMEM((2, 12 * 128, 256), bf16),
         pltpu.VMEM((2, 12 * 128, 256), bf16),
-        pltpu.VMEM((2 * 8 * max(STEP), 12 * 128), bf16),
+        pltpu.VMEM((640, 12 * 128), bf16),
         pltpu.VMEM((2 * DIMS, 8, 128), f32),
         pltpu.VMEM((128, 128), f32),
         pltpu.VMEM((8, 128), jnp.int32),

time: 94.5 us -> 85.5 us (0.905)
  Pallas kernels: 90.5 us -> 81.6 us
    pallas_call x1, Pallas kernels: 90.5 us -> 81.6 us  [on_device(): pl.pallas_call(functools.partial(kernel, ns), out_shape=jax.ShapeDtypeStr...]
where the time goes in v3:
time: 85.5 us; the launch traced here: 83.9 us
  Pallas kernels  81.6 us (95%)
  local copies, waits for them, and re-layouts  2.34 us (3%)
    pallas_call x1, Pallas kernels, on_device(): pl.pallas_call(functools.partial(kernel, ns), out_shape=jax.ShapeDtypeStr...  81.6 us
    unnamed x1, local copies, waits for them, and re-layouts  2.34 us

profile of v3, /device:TPU:1, one launch (start us, length us, event | category | flops | bytes accessed | tf_op | source)
XLA Modules:
  0.0 83.9 jit_solution(13871016989348065159)
XLA Ops:
  0.0 81.6 %shard_map.64 = f32[2112,128]{1,0:T(8,128)} custom-call(f32[2112,128]{1,0:T(8,128)} %bitcast.5, f32[5,2,32,128]{3,2,1,0:T(8,128)} %fl.1, f32[5,126]{1,0:T(8,128)} %bitcast.7, s32[630]{0:T(1024)} %constant.2.clone.ptab, s32[176]{0:T(256)} %slots.1, f32[3,3,27]{2,1,0:T(4,128)} %bitcast.6), custom_call_target="tpu_custom_call" | custom-call | tf_op jit(solution)/shard_map/pallas_call | solution.py:559
  81.6 2.3 %copy.8 = f32[11,3,2,32,128]{4,3,2,1,0:T(8,128)} copy(f32[11,3,2,32,128]{4,3,2,1,0:T(8,128)} %bitcast.4) | data formatting | bytes 2162688

commit v4 on v3

--- a/solution.py
+++ b/solution.py
@@ -17,9 +17,11 @@
 CAP = (1, 1, 1, 3, 5)
 BASE = (0, 1, 2, 3, 6)
 T8 = (8, 8, 16, 40, 72)
-STEP = (2, 6, 16, 36, 36)
+STEP = (2, 6, 16, 0, 0)
+PARTS = (((0, 1, 8),), ((0, 5, 8),), ((0, 15, 16),), ((0, 16, 16), (16, 19, 24)), ((0, 32, 32), (32, 38, 40)))
 WIDE = (True, True, True, False, False)
 CHUNKS = ((0, 1), (1, 2), (3, 3), (6, 5))
+OUTS = ((0, 1, (0, 1)), (1, 2, (0, 1)), (3, 3, (0, 1)), (6, 5, (0,)), (6, 5, (1,)))
 CHUNK_OF = ((0, 0), (1, 0), (1, 1), (2, 0), (3, 0))
 DIRS = tuple((dx, dz) for dx in (-1, 0, 1) for dz in (-1, 0, 1) if (dx, dz) != (0, 0))
 MESH = pl.DeviceIdType.MESH
@@ -61,15 +63,15 @@
     it = iter(scr)
     sb = [next(it) for _ in CHUNKS]
     rb = [next(it) for _ in CHUNKS]
-    ob = [next(it) for _ in CHUNKS]
-    qb = [next(it) for _ in CHUNKS]
+    ob = [next(it) for _ in OUTS]
+    qb = [next(it) for _ in OUTS]
     load_buf = [next(it) for _ in range(5)]
     sett_buf = [next(it) for _ in range(4)]
     own_buf = [next(it) for _ in range(5)]
     img_buf = [next(it) for _ in range(4)]
     faces = [next(it) for _ in range(9)]
     rims = [next(it) for _ in range(9)]
-    wh, wl, xs, ff, ft, posv, pos, pos_sem = [next(it) for _ in range(8)]
+    wh, wl, wc, xs, ff, ft, posv, pos, pos_sem = [next(it) for _ in range(9)]
     in_s, in_r, out_s, out_r, h_s, h_r = [next(it) for _ in range(6)]
 
     s = lax.axis_index("space")
@@ -182,13 +184,10 @@
     to_smem = pltpu.make_async_copy(posv, pos, pos_sem)
     to_smem.start()
 
-    for dz in range(3):
-        for which in range(2):
-            for w in (wh, wl):
-                w[which, (dz * 4 + 3) * 128 : (dz * 4 + 4) * 128, 0:128] = jnp.zeros(
-                    (128, 128), jnp.bfloat16
-                )
-                w[which, dz * 512 : dz * 512 + 128, 128:256] = jnp.zeros((128, 128), jnp.bfloat16)
+    for which in range(2):
+        for w in (wh, wl):
+            w[which, 9 * 128 :, 0:128] = jnp.zeros((384, 128), jnp.bfloat16)
+            w[which, 0 : 3 * 128, 128:256] = jnp.zeros((384, 128), jnp.bfloat16)
     lane1 = lax.broadcasted_iota(jnp.int32, (1, 128), 1)
     group = lane1 // 32
 
@@ -223,8 +222,12 @@
             for which in range(2):
                 hi = block[which].astype(jnp.bfloat16)
                 lo = (block[which] - hi.astype(jnp.float32)).astype(jnp.bfloat16)
+                if which == 0:
+                    row = pl.multiple_of((dx * 3 + dz) * 128 + b * 32, 32)
+                    wc[pl.ds(row, 32), 0:128] = hi
+                    wc[pl.ds(row, 32), 128:256] = lo
                 for px in range(2):
-                    row = pl.multiple_of((dz * 4 + dx + px) * 128 + b * 32, 32)
+                    row = pl.multiple_of(((dx + px) * 3 + dz) * 128 + b * 32, 32)
                     wh[which, pl.ds(row, 32), px * 128 : px * 128 + 128] = hi
                     wl[which, pl.ds(row, 32), px * 128 : px * 128 + 128] = lo
         return 0
@@ -276,58 +279,65 @@
     pack(3)
     to_smem.wait()
 
-    def halo_copy(e, n, buf, count):
+    def halo_copy(q, n, e, buf, part):
+        t0, count, n8 = part
         dx, dz = DIRS[n]
         sx, tx = {1: (2, 0), -1: (1, 3), 0: (0, 0)}[dx]
         if buf.shape[0] == 6:
             tx = {1: 0, -1: 4, 0: 2}[dx]
             if dz == 0:
-                src, dst = buf.at[2:4, 0:count, 8:16, :], buf.at[tx : tx + 2, 0:count, 8:16, :]
+                src = buf.at[2:4, t0 : t0 + count, 8:16, :]
+                dst = buf.at[tx : tx + 2, t0 : t0 + count, 8:16, :]
             else:
                 side = 1 if dz > 0 else 0
                 src = faces[e].at[side]
                 dst = rims[e].at[1 - side, 1 - side : 3 - side, tx : tx + 2]
         elif dz == 0:
-            src, dst = buf.at[sx, 0:count, 8:16, :], buf.at[tx, 0:count, 8:16, :]
+            src = buf.at[sx, t0 : t0 + count, 8:16, :]
+            dst = buf.at[tx, t0 : t0 + count, 8:16, :]
         else:
             side = 1 if dz > 0 else 0
             if dx == 0:
-                src, dst = faces[e].at[side], rims[e].at[1 - side, 1:3]
+                src = faces[e].at[side, :, t0 : t0 + n8]
+                dst = rims[e].at[1 - side, 1:3, t0 : t0 + n8]
             else:
-                src, dst = faces[e].at[side, sx - 1], rims[e].at[1 - side, tx]
+                src = faces[e].at[side, sx - 1, t0 : t0 + n8]
+                dst = rims[e].at[1 - side, tx, t0 : t0 + n8]
         return pltpu.make_async_remote_copy(
             src_ref=src,
             dst_ref=dst,
-            send_sem=h_s.at[e, n],
-            recv_sem=h_r.at[e, n],
+            send_sem=h_s.at[q, n],
+            recv_sem=h_r.at[q, n],
             device_id={"space": s + dx, "terms": term_of(i + dz)},
             device_id_type=MESH,
         )
 
-    def by_five(count, fn):
-        w = min(count, 5)
+    def by_five(part, fn):
+        t0, count, _ = part
+        w = next(w for w in (5, 4, 1) if count % w == 0) if count != 19 and count != 38 else 19
 
         def some(u, _):
             for v in range(w):
-                fn(u * w + v)
+                fn(t0 + u * w + v)
             return 0
 
         lax.fori_loop(0, count // w, some, 0)
 
     exchanges = []
 
-    def start_exchange(e, buf, count):
-        exchanges.append((e, buf, count))
+    def start_exchange(e, buf, part):
+        args = (len(exchanges), e, buf, part)
+        exchanges.append(args)
         for n, (dx, dz) in enumerate(DIRS):
-            pl.when(inside(dx, dz))(lambda n=n: halo_copy(e, n, buf, count).start())
-
-    def end_exchange(e, buf, count):
+            pl.when(inside(dx, dz))(lambda n=n: halo_copy(args[0], n, *args[1:]).start())
+        return args
+
+    def end_exchange(q, e, buf, part):
         for n, (dx, dz) in enumerate(DIRS):
-            pl.when(inside(-dx, -dz))(lambda n=n: halo_copy(e, n, buf, count).wait_recv())
-
-        spread_rim(e, buf, count)
-
-    def spread_rim(e, buf, count):
+            pl.when(inside(-dx, -dz))(lambda n=n: halo_copy(q, n, e, buf, part).wait_recv())
+        spread_rim(e, buf, part)
+
+    def spread_rim(e, buf, part):
         def spread(t):
             for x in range(4):
                 buf[x, t, 7:8, :] = rims[e][0, x, pl.ds(t, 1), :]
@@ -340,7 +350,7 @@
                 rims[e][0, 2, x, pl.ds(t, 1), :] = buf[x, t, 8:9, :]
                 rims[e][1, 0, x, pl.ds(t, 1), :] = buf[x, t, 15:16, :]
 
-        by_five(count, spread_wide if buf.shape[0] == 6 else spread)
+        by_five(part, spread_wide if buf.shape[0] == 6 else spread)
 
     def halves(v):
         hi = v.astype(jnp.bfloat16)
@@ -365,7 +375,7 @@
                 for w in range(4):
                     for b in range(2):
                         v = [src[2 * b + w, 2 * u + h, 7 + dz : 15 + dz, :] for h in range(2)]
-                        put(b * 8 * step + u * 16, (dz * 4 + w) * 128, jnp.concatenate(v, axis=0))
+                        put(b * 8 * step + u * 16, (w * 3 + dz) * 128, jnp.concatenate(v, axis=0))
             return 0
 
         lax.fori_loop(0, step // 2, pair, 0)
@@ -373,7 +383,7 @@
             for dz in range(3):
                 for w in range(4):
                     v = [rim[side, dz, 2 * b + w] for b in range(2)]
-                    put(base + side * 2 * t8, (dz * 4 + w) * 128, jnp.concatenate(v, axis=0))
+                    put(base + side * 2 * t8, (w * 3 + dz) * 128, jnp.concatenate(v, axis=0))
         res = product(rows, 0)
         one, zero = jnp.float32(1.0), jnp.float32(0.0)
         in_x = [jnp.where(s > 0, one, zero), one, one, jnp.where(s < ns - 1, one, zero)]
@@ -390,36 +400,34 @@
                 row = base + side * 2 * t8 + b * t8
                 rims[2 * lv + 1][side, x] = res[row : row + t8, lanes] * (in_x[x] * in_z[side])
 
-    def apply(lv, src, which, store):
-        step = STEP[lv]
-        rows = step * 8
-
-        def chunk(ci, _):
-            def pair(u, _):
-                t = ci * step + 2 * u
-                for dz in range(3):
-                    for x in range(4):
-                        v = jnp.concatenate(
-                            [src[x, t, 7 + dz : 15 + dz, :], src[x, t + 1, 7 + dz : 15 + dz, :]], axis=0
-                        )
-                        hi, lo = halves(v)
-                        col = (dz * 4 + x) * 128
-                        xs[pl.ds(pl.multiple_of(u * 16, 16), 16), col : col + 128] = hi
-                        xs[pl.ds(pl.multiple_of(rows + u * 16, 16), 16), col : col + 128] = lo
-                return 0
-
-            lax.fori_loop(0, step // 2, pair, 0)
-            res = product(rows, which)
-            for px in range(2):
-                store(px, ci * step, res[:, px * 128 : px * 128 + 128].reshape(step, 8, 128))
+    def stage_rows(src, part, lo_at, at=0):
+        t0, count, _ = part
+
+        def pair(u, _):
+            t = t0 + 2 * u
+            for dz in range(3):
+                for x in range(4):
+                    v = jnp.concatenate(
+                        [src[x, t, 7 + dz : 15 + dz, :], src[x, t + 1, 7 + dz : 15 + dz, :]], axis=0
+                    )
+                    hi, lo = halves(v)
+                    col = (x * 3 + dz) * 128
+                    xs[pl.ds(pl.multiple_of(at + u * 16, 16), 16), col : col + 128] = hi
+                    xs[pl.ds(pl.multiple_of(lo_at + u * 16, 16), 16), col : col + 128] = lo
             return 0
 
-        lax.fori_loop(0, -(-COUNT[lv] // step), chunk, 0)
+        lax.fori_loop(0, (count + 1) // 2, pair, 0)
+
+    def apply(src, part, which, store):
+        step = (part[1] + 1) // 2 * 2
+        stage_rows(src, part, 8 * step)
+        res = product(8 * step, which)
+        for px in range(2):
+            store(px, part[0], res[:, px * 128 : px * 128 + 128].reshape(step, 8, 128))
 
     pending = []
     for lv in range(5):
         c, j0 = CHUNK_OF[lv]
-        step = STEP[lv]
         if lv == 0 or c != CHUNK_OF[lv - 1][0]:
             wait_in(c)
         if lv == 0:
@@ -447,85 +455,100 @@
                     faces[2 * lv][0, x, pl.ds(t, 1), :] = parts[x][0:1]
                     faces[2 * lv][1, x, pl.ds(t, 1), :] = parts[x][7:8]
 
-        by_five(COUNT[lv], load_of)
-        start_exchange(2 * lv, load_buf[lv], COUNT[lv])
+        started = []
+        for part in PARTS[lv]:
+            by_five(part, load_of)
+            started.append(start_exchange(2 * lv, load_buf[lv], part))
         if pending:
             pending.pop()()
-        end_exchange(2 * lv, load_buf[lv], COUNT[lv])
         if lv == 1:
             send_in(3)
 
+        def deliver_to(o, j0, layers, lv=lv):
+            def deliver(g, _):
+                for j in range(CAP[lv]):
+                    q = slots[g * SLOT_DEV + BASE[lv] + j]
+                    t = jnp.clip(q - START[lv], 0, COUNT[lv] - 1)
+                    for n, x in enumerate(layers):
+                        v = own_buf[lv][x, t]
+                        ob[o][g, len(layers) * (j0 + j) + n] = jnp.where(q >= 0, v, 0.0)
+                return 0
+
+            lax.fori_loop(0, GROUPS, deliver, 0)
+
+        def face(t):
+            for x in range(2):
+                faces[2 * lv + 1][0, x, pl.ds(t, 1), :] = sett_buf[lv][1 + x, t, 8:9, :]
+                faces[2 * lv + 1][1, x, pl.ds(t, 1), :] = sett_buf[lv][1 + x, t, 15:16, :]
+
         def settle(px, t0, v):
-            own_buf[lv][px, pl.ds(t0, step)] = v
-            if lv < 4:
-                sett_buf[lv][1 + px, pl.ds(t0, step), 8:16, :] = v
+            own_buf[lv][px, t0 : t0 + v.shape[0]] = v
+            sett_buf[lv][1 + px, t0 : t0 + v.shape[0], 8:16, :] = v
+
+        def image(px, t0, v):
+            img_buf[lv][px, t0 : t0 + v.shape[0]] = v
 
         if WIDE[lv]:
+            end_exchange(*started[0])
             settle_wide(lv)
-            spread_rim(2 * lv + 1, sett_buf[lv], COUNT[lv])
+            spread_rim(2 * lv + 1, sett_buf[lv], PARTS[lv][0])
+            apply(sett_buf[lv], PARTS[lv][0], 1, image)
+
+            def finish(lv=lv, c=c, j0=j0, deliver_to=deliver_to):
+                deliver_to(c, j0, (0, 1))
+                if CHUNK_OF[lv + 1][0] != c:
+                    send_out(c)
+
+            pending.append(finish)
+        elif lv < 4:
+            rimmed = []
+            for part, args in zip(PARTS[lv], started):
+                end_exchange(*args)
+                apply(load_buf[lv], part, 0, settle)
+                by_five(part, face)
+                rimmed.append(start_exchange(2 * lv + 1, sett_buf[lv], part))
+            deliver_to(c, j0, (0, 1))
+            for part, args in zip(PARTS[lv], rimmed):
+                end_exchange(*args)
+                apply(sett_buf[lv], part, 1, image)
+            send_out(c)
         else:
-            apply(lv, load_buf[lv], 0, settle)
-
-        if lv < 4 and not WIDE[lv]:
-            def face(t):
-                for x in range(2):
-                    faces[2 * lv + 1][0, x, pl.ds(t, 1), :] = sett_buf[lv][1 + x, t, 8:9, :]
-                    faces[2 * lv + 1][1, x, pl.ds(t, 1), :] = sett_buf[lv][1 + x, t, 15:16, :]
-
-            by_five(COUNT[lv], face)
-            start_exchange(2 * lv + 1, sett_buf[lv], COUNT[lv])
-
-        def deliver(g, _, lv=lv, c=c, j0=j0):
-            for j in range(CAP[lv]):
-                q = slots[g * SLOT_DEV + BASE[lv] + j]
-                t = jnp.clip(q - START[lv], 0, COUNT[lv] - 1)
-                for x in range(2):
-                    v = own_buf[lv][x, t]
-                    ob[c][g, 2 * (j0 + j) + x] = jnp.where(q >= 0, v, 0.0)
-            return 0
-
-        if not WIDE[lv]:
-            lax.fori_loop(0, GROUPS, deliver, 0)
-
-        if lv < 4:
-            if not WIDE[lv]:
-                end_exchange(2 * lv + 1, sett_buf[lv], COUNT[lv])
-
-            def image(px, t0, v):
-                img_buf[lv][px, pl.ds(t0, step)] = v
-
-            apply(lv, sett_buf[lv], 1, image)
-
-        def finish(lv=lv, c=c, deliver=deliver):
-            if WIDE[lv]:
-                lax.fori_loop(0, GROUPS, deliver, 0)
-            if lv == 4 or CHUNK_OF[lv + 1][0] != c:
-                send_out(c)
-
-        if WIDE[lv]:
-            pending.append(finish)
-        else:
-            finish()
-
-    for c, (j0, n) in enumerate(CHUNKS):
+            lo_at = 8 * COUNT[lv]
+            for px in range(2):
+                for part, args in zip(PARTS[lv], started):
+                    at, n = 8 * part[0], 8 * part[1]
+                    if px == 0:
+                        end_exchange(*args)
+                        stage_rows(load_buf[lv], part, lo_at + at, at)
+                    cols = slice(384 * px, 384 * px + 1152)
+                    wide = dot(xs[at : at + n, cols], wc[...])
+                    res = dot(xs[lo_at + at : lo_at + at + n, cols], wc[:, 0:128])
+                    res = res + wide[:, 0:128] + wide[:, 128:256]
+                    own_buf[lv][px, part[0] : part[0] + part[1]] = res.reshape(part[1], 8, 128)
+                deliver_to(3 + px, 0, (px,))
+                send_out(3 + px)
+
+    for c, (j0, n, layers) in enumerate(OUTS):
         wait_out(c)
 
-        def unpack(m, _, c=c, j0=j0):
-            j, x = j0 + m // 2, m % 2
+        def unpack(m, _, c=c, j0=j0, layers=layers):
+            j = j0 + m // len(layers)
+            x = m % 2 if len(layers) == 2 else layers[0]
             turned = jnp.transpose(qb[c][:, m].reshape(128, 128))
             for a in range(3):
                 row = pl.multiple_of((j * 6 + a * 2 + x) * 32, 32)
                 out[pl.ds(row, 32), :] = turned[32 * a : 32 * a + 32]
             return 0
 
-        lax.fori_loop(0, 2 * n, unpack, 0)
+        lax.fori_loop(0, len(layers) * n, unpack, 0)
 
     for c in range(len(CHUNKS)):
         over_peers(lambda p: leaving(c, p, sb[c], rb[c], in_s, in_r, True).wait_send())
+    for c in range(len(OUTS)):
         over_peers(lambda p: leaving(c, p, ob[c], qb[c], out_s, out_r, False).wait_send())
-    for e, buf, count in exchanges:
+    for q, e, buf, part in exchanges:
         for n, (dx, dz) in enumerate(DIRS):
-            pl.when(inside(dx, dz))(lambda n=n: halo_copy(e, n, buf, count).wait_send())
+            pl.when(inside(dx, dz))(lambda n=n: halo_copy(q, n, e, buf, part).wait_send())
 
 
 def on_device(ns, forcing, stencil, fields, coupling, slot_term):
@@ -534,7 +557,10 @@
     sm = pl.BlockSpec(memory_space=pltpu.SMEM)
     f32, bf16 = jnp.float32, jnp.bfloat16
     dma = pltpu.SemaphoreType.DMA
-    scratch = [pltpu.VMEM((GROUPS, 2 * n, 8, 128), f32) for _ in range(4) for _, n in CHUNKS]
+    scratch = [pltpu.VMEM((GROUPS, 2 * n, 8, 128), f32) for _ in range(2) for _, n in CHUNKS]
+    scratch += [
+        pltpu.VMEM((GROUPS, len(x) * n, 8, 128), f32) for _ in range(2) for _, n, x in OUTS
+    ]
     scratch += [pltpu.VMEM((6 if WIDE[lv] else 4, T8[lv], 24, 128), f32) for lv in range(5)]
     scratch += [pltpu.VMEM((4, T8[lv], 24, 128), f32) for lv in range(4)]
     scratch += [pltpu.VMEM((2, T8[lv], 8, 128), f32) for lv in range(5)]
@@ -548,14 +574,16 @@
     scratch += [
         pltpu.VMEM((2, 12 * 128, 256), bf16),
         pltpu.VMEM((2, 12 * 128, 256), bf16),
-        pltpu.VMEM((640, 12 * 128), bf16),
+        pltpu.VMEM((9 * 128, 256), bf16),
+        pltpu.VMEM((16 * COUNT[4], 12 * 128), bf16),
         pltpu.VMEM((2 * DIMS, 8, 128), f32),
         pltpu.VMEM((128, 128), f32),
         pltpu.VMEM((8, 128), jnp.int32),
         pltpu.SMEM((8, 128), jnp.int32),
         dma(()),
     ]
-    scratch += [dma((len(CHUNKS), GROUPS)) for _ in range(4)] + [dma((9, 8)) for _ in range(2)]
+    scratch += [dma((len(CHUNKS), GROUPS)) for _ in range(2)]
+    scratch += [dma((len(OUTS), GROUPS)) for _ in range(2)] + [dma((9, 8)) for _ in range(2)]
     out = pl.pallas_call(
         functools.partial(kernel, ns),
         out_shape=jax.ShapeDtypeStruct((rows, 128), f32),
@@ -563,7 +591,7 @@
         out_specs=vm,
         scratch_shapes=scratch,
         compiler_params=pltpu.CompilerParams(
-            collective_id=0, has_side_effects=True, vmem_limit_bytes=56 << 20
+            collective_id=0, has_side_effects=True, vmem_limit_bytes=32 << 20
         ),
     )(forcing.reshape(rows, 128), fields, coupling.T, jnp.asarray(parent_table()), slot_term, stencil.transpose(1, 2, 0))
     return out.reshape(forcing.shape)

time: 85.5 us -> 84.6 us (0.989); the launches traced: 83.9 us -> 84.3 us
  local copies, waits for them, and re-layouts: 2.34 us -> 5.88 us
  Pallas kernels: 81.6 us -> 78.4 us
    unnamed x1 -> x13, local copies, waits for them, and re-layouts: 2.34 us -> 5.88 us
    pallas_call x1, Pallas kernels: 81.6 us -> 78.4 us  [on_device(): pl.pallas_call(functools.partial(kernel, ns), out_shape=jax.ShapeDtypeStr...]
where the time goes in v4:
time: 84.6 us; the launch traced here: 84.3 us
  Pallas kernels  78.4 us (93%)
  local copies, waits for them, and re-layouts  5.88 us (7%)
    pallas_call x1, Pallas kernels, on_device(): pl.pallas_call(functools.partial(kernel, ns), out_shape=jax.ShapeDtypeStr...  78.4 us
    unnamed x13, local copies, waits for them, and re-layouts  5.88 us

profile of v4, /device:TPU:1, one launch (start us, length us, event | category | flops | bytes accessed | tf_op | source)
XLA Modules:
  0.0 84.3 jit_solution(9700913220532917462)
XLA Ops:
  0.0 0.0 copy-start
  0.0 1.2 %copy-done = f32[11,3,2,32,128]{4,3,2,1,0:T(8,128)S(1)} copy-done((f32[11,3,2,32,128]{4,3,2,1,0:T(8,128)S(1)}, f32[11,3,2,32,128]{4,3,2,1,0:T(8,128)}, u32[]{:S(2)}) %copy-start) | copy-done | bytes 1081368
  1.2 0.0 copy-start.1
  1.2 0.9 %copy-done.1 = f32[5,2,32,128]{3,2,1,0:T(8,128)S(1)} copy-done((f32[5,2,32,128]{3,2,1,0:T(8,128)S(1)}, f32[5,2,32,128]{3,2,1,0:T(8,128)}, u32[]{:S(2)}) %copy-start.1) | copy-done | bytes 163864
  2.2 0.0 copy-start.2
  2.2 0.7 copy-done.2
  2.8 0.0 copy-start.3
  2.8 0.7 copy-done.3
  3.5 0.0 copy-start.4
  3.5 0.7 copy-done.4
  4.2 0.0 copy-start.5
  4.2 0.7 copy-done.5
  4.9 78.4 %shard_map.64 = f32[2112,128]{1,0:T(8,128)S(1)} custom-call(f32[2112,128]{1,0:T(8,128)S(1)} %bitcast.5, f32[5,2,32,128]{3,2,1,0:T(8,128)S(1)} %copy-done.1, f32[5,126]{1,0:T(8,128)S(1)} %bitcast.7, s32[630]{0:T(1024)S(1)} %copy-done.4, s32[176]{0:T(256)S(1)} %copy-done.5, f32[3,3,27]{2,1,0:T(4,128)S(1)} %bitcast.6), custom_call_target="tpu_custom_call" | custom-call | tf_op jit(solution)/shard_map/pallas_call | solution.py:587
  83.3 1.0 %copy.8 = f32[11,3,2,32,128]{4,3,2,1,0:T(8,128)} copy(f32[11,3,2,32,128]{4,3,2,1,0:T(8,128)S(1)} %bitcast.4) | data formatting | bytes 2162688
Async XLA Ops:
  0.0 1.2 %copy-start = (f32[11,3,2,32,128]{4,3,2,1,0:T(8,128)S(1)}, f32[11,3,2,32,128]{4,3,2,1,0:T(8,128)}, u32[]{:S(2)}) copy-start(f32[11,3,2,32,128]{4,3,2,1,0:T(8,128)} %param.6) | copy-start | bytes 3244036
  1.2 0.9 %copy-start.1 = (f32[5,2,32,128]{3,2,1,0:T(8,128)S(1)}, f32[5,2,32,128]{3,2,1,0:T(8,128)}, u32[]{:S(2)}) copy-start(f32[5,2,32,128]{3,2,1,0:T(8,128)} %fl.1) | copy-start | bytes 491524
  2.2 0.7 copy-start.2
  2.8 0.7 copy-start.3
  3.5 0.7 copy-start.4
  4.2 0.7 copy-start.5

commit v5 on v4

--- a/solution.py
+++ b/solution.py
@@ -59,8 +59,15 @@
     return q * 4 + r + (q % 2) * (3 - 2 * r)
 
 
-def kernel(ns, fin, fl, cp, ptab, slots, sten, out, *scr):
-    it = iter(scr)
+def kernel(ns, *refs):
+    given, out, it = refs[:6], refs[6], iter(refs[7:])
+    fin, fl, cp, ptab, slots, sten, given_sem = [next(it) for _ in range(7)]
+    fetch = [
+        pltpu.make_async_copy(src, dst, given_sem.at[n])
+        for n, (src, dst) in enumerate(zip(given, (fin, fl, cp, ptab, slots, sten)))
+    ]
+    for copy in fetch:
+        copy.start()
     sb = [next(it) for _ in CHUNKS]
     rb = [next(it) for _ in CHUNKS]
     ob = [next(it) for _ in OUTS]
@@ -71,7 +78,7 @@
     img_buf = [next(it) for _ in range(4)]
     faces = [next(it) for _ in range(9)]
     rims = [next(it) for _ in range(9)]
-    wh, wl, wc, xs, ff, ft, posv, pos, pos_sem = [next(it) for _ in range(9)]
+    wh, wc, xs, low, ff, ft, posv, pos, pos_sem = [next(it) for _ in range(9)]
     in_s, in_r, out_s, out_r, h_s, h_r = [next(it) for _ in range(6)]
 
     s = lax.axis_index("space")
@@ -167,12 +174,15 @@
     def wait_out(c):
         over_peers(lambda p: arriving(c, p, ob[c], qb[c], out_s, out_r, False).wait_recv())
 
+    fetch[0].wait()
     pack(0)
     wait_barrier()
     send_in(0)
     pack(1)
     send_in(1)
 
+    for copy in fetch[1:]:
+        copy.wait()
     lane8 = lax.broadcasted_iota(jnp.int32, (8, 128), 1)
 
     def locate(g, acc):
@@ -185,9 +195,8 @@
     to_smem.start()
 
     for which in range(2):
-        for w in (wh, wl):
-            w[which, 9 * 128 :, 0:128] = jnp.zeros((384, 128), jnp.bfloat16)
-            w[which, 0 : 3 * 128, 128:256] = jnp.zeros((384, 128), jnp.bfloat16)
+        wh[which, 9 * 128 :, 0:128] = jnp.zeros((384, 128), jnp.bfloat16)
+        wh[which, 0 : 3 * 128, 128:256] = jnp.zeros((384, 128), jnp.bfloat16)
     lane1 = lax.broadcasted_iota(jnp.int32, (1, 128), 1)
     group = lane1 // 32
 
@@ -222,14 +231,12 @@
             for which in range(2):
                 hi = block[which].astype(jnp.bfloat16)
                 lo = (block[which] - hi.astype(jnp.float32)).astype(jnp.bfloat16)
-                if which == 0:
-                    row = pl.multiple_of((dx * 3 + dz) * 128 + b * 32, 32)
-                    wc[pl.ds(row, 32), 0:128] = hi
-                    wc[pl.ds(row, 32), 128:256] = lo
+                row = pl.multiple_of((dx * 3 + dz) * 128 + b * 32, 32)
+                wc[which, pl.ds(row, 32), 0:128] = hi
+                wc[which, pl.ds(row, 32), 128:256] = lo
                 for px in range(2):
                     row = pl.multiple_of(((dx + px) * 3 + dz) * 128 + b * 32, 32)
                     wh[which, pl.ds(row, 32), px * 128 : px * 128 + 128] = hi
-                    wl[which, pl.ds(row, 32), px * 128 : px * 128 + 128] = lo
         return 0
 
     lax.fori_loop(0, 9, table, 0)
@@ -357,8 +364,12 @@
         return hi, (v - hi.astype(jnp.float32)).astype(jnp.bfloat16)
 
     def product(rows, which):
-        both = dot(xs[0 : 2 * rows, :], wh[which])
-        return both[0:rows] + both[rows:] + dot(xs[0:rows, :], wl[which])
+        rest = dot(xs[rows : 2 * rows, :], wh[which])
+        return [main(0, rows, px, which) + rest[:, 128 * px : 128 * px + 128] for px in range(2)]
+
+    def main(at, rows, px, which):
+        both = dot(xs[at : at + rows, 384 * px : 384 * px + 1152], wc[which])
+        return both[:, 0:128] + both[:, 128:256]
 
     def settle_wide(lv):
         src, rim, step, t8 = load_buf[lv], rims[2 * lv], STEP[lv], T8[lv]
@@ -389,8 +400,8 @@
         in_x = [jnp.where(s > 0, one, zero), one, one, jnp.where(s < ns - 1, one, zero)]
         in_z = [jnp.where(i > 0, one, zero), jnp.where(i < GROUPS - 1, one, zero)]
         for x in range(4):
-            b, lanes = x // 2, slice(128 * (x % 2), 128 * (x % 2) + 128)
-            v = res[b * 8 * step : (b + 1) * 8 * step, lanes].reshape(step, 8, 128)
+            b, mine = x // 2, res[x % 2]
+            v = mine[b * 8 * step : (b + 1) * 8 * step].reshape(step, 8, 128)
             if x in (1, 2):
                 own_buf[lv][x - 1, 0:step] = v
             else:
@@ -398,7 +409,7 @@
             sett_buf[lv][x, 0:step, 8:16, :] = v
             for side in range(2):
                 row = base + side * 2 * t8 + b * t8
-                rims[2 * lv + 1][side, x] = res[row : row + t8, lanes] * (in_x[x] * in_z[side])
+                rims[2 * lv + 1][side, x] = mine[row : row + t8] * (in_x[x] * in_z[side])
 
     def stage_rows(src, part, lo_at, at=0):
         t0, count, _ = part
@@ -423,7 +434,7 @@
         stage_rows(src, part, 8 * step)
         res = product(8 * step, which)
         for px in range(2):
-            store(px, part[0], res[:, px * 128 : px * 128 + 128].reshape(step, 8, 128))
+            store(px, part[0], res[px].reshape(step, 8, 128))
 
     pending = []
     for lv in range(5):
@@ -476,6 +487,22 @@
 
             lax.fori_loop(0, GROUPS, deliver, 0)
 
+        def deliver_packed(o, x, lv=lv):
+            def deliver(g, _):
+                v = []
+                for j in range(CAP[lv]):
+                    q = slots[g * SLOT_DEV + BASE[lv] + j]
+                    t = jnp.clip(q - START[lv], 0, COUNT[lv] - 1)
+                    v.append(jnp.where(q >= 0, own_buf[lv][x, t], 0.0))
+                r1, r2, r3 = [pltpu.roll(v[1 + n], 96 - 32 * n, 1) for n in range(3)]
+                ob[o][g, 0] = jnp.where(lane8 < 96, v[0], r1)
+                ob[o][g, 1] = jnp.where(lane8 < 64, r1, r2)
+                ob[o][g, 2] = jnp.where(lane8 < 32, r2, r3)
+                ob[o][g, 3] = v[4]
+                return 0
+
+            lax.fori_loop(0, GROUPS, deliver, 0)
+
         def face(t):
             for x in range(2):
                 faces[2 * lv + 1][0, x, pl.ds(t, 1), :] = sett_buf[lv][1 + x, t, 8:9, :]
@@ -520,27 +547,31 @@
                     if px == 0:
                         end_exchange(*args)
                         stage_rows(load_buf[lv], part, lo_at + at, at)
-                    cols = slice(384 * px, 384 * px + 1152)
-                    wide = dot(xs[at : at + n, cols], wc[...])
-                    res = dot(xs[lo_at + at : lo_at + at + n, cols], wc[:, 0:128])
-                    res = res + wide[:, 0:128] + wide[:, 128:256]
+                        low[at : at + n, :] = dot(xs[lo_at + at : lo_at + at + n, :], wh[0])
+                    res = main(at, n, px, 0) + low[at : at + n, 128 * px : 128 * px + 128]
                     own_buf[lv][px, part[0] : part[0] + part[1]] = res.reshape(part[1], 8, 128)
-                deliver_to(3 + px, 0, (px,))
+                deliver_packed(3 + px, px)
                 send_out(3 + px)
 
     for c, (j0, n, layers) in enumerate(OUTS):
         wait_out(c)
+        if len(layers) == 1:
+            for m in range(4):
+                turned = jnp.transpose(qb[c][:, m].reshape(128, 128))
+                for g in range(4 * m, min(4 * m + 4, 15)):
+                    row = ((j0 + g // 3) * 6 + g % 3 * 2 + layers[0]) * 32
+                    out[row : row + 32, :] = turned[32 * (g - 4 * m) : 32 * (g - 4 * m) + 32]
+            continue
 
         def unpack(m, _, c=c, j0=j0, layers=layers):
-            j = j0 + m // len(layers)
-            x = m % 2 if len(layers) == 2 else layers[0]
+            j, x = j0 + m // 2, m % 2
             turned = jnp.transpose(qb[c][:, m].reshape(128, 128))
             for a in range(3):
                 row = pl.multiple_of((j * 6 + a * 2 + x) * 32, 32)
                 out[pl.ds(row, 32), :] = turned[32 * a : 32 * a + 32]
             return 0
 
-        lax.fori_loop(0, len(layers) * n, unpack, 0)
+        lax.fori_loop(0, 2 * n, unpack, 0)
 
     for c in range(len(CHUNKS)):
         over_peers(lambda p: leaving(c, p, sb[c], rb[c], in_s, in_r, True).wait_send())
@@ -554,12 +585,21 @@
 def on_device(ns, forcing, stencil, fields, coupling, slot_term):
     rows = forcing.shape[0] * 6 * 32
     vm = pl.BlockSpec(memory_space=pltpu.VMEM)
-    sm = pl.BlockSpec(memory_space=pltpu.SMEM)
+    hbm = pl.BlockSpec(memory_space=pltpu.HBM)
     f32, bf16 = jnp.float32, jnp.bfloat16
     dma = pltpu.SemaphoreType.DMA
-    scratch = [pltpu.VMEM((GROUPS, 2 * n, 8, 128), f32) for _ in range(2) for _, n in CHUNKS]
+    scratch = [
+        pltpu.VMEM((rows, 128), f32),
+        pltpu.VMEM(fields.shape, f32),
+        pltpu.SMEM(coupling.shape[::-1], f32),
+        pltpu.SMEM((TERMS * DIMS,), jnp.int32),
+        pltpu.SMEM(slot_term.shape, jnp.int32),
+        pltpu.SMEM((3, 3, 27), f32),
+        dma((6,)),
+    ]
+    scratch += [pltpu.VMEM((GROUPS, 2 * n, 8, 128), f32) for _ in range(2) for _, n in CHUNKS]
     scratch += [
-        pltpu.VMEM((GROUPS, len(x) * n, 8, 128), f32) for _ in range(2) for _, n, x in OUTS
+        pltpu.VMEM((GROUPS, 2 * n if len(x) == 2 else 4, 8, 128), f32) for _ in range(2) for _, n, x in OUTS
     ]
     scratch += [pltpu.VMEM((6 if WIDE[lv] else 4, T8[lv], 24, 128), f32) for lv in range(5)]
     scratch += [pltpu.VMEM((4, T8[lv], 24, 128), f32) for lv in range(4)]
@@ -573,9 +613,9 @@
     ]
     scratch += [
         pltpu.VMEM((2, 12 * 128, 256), bf16),
-        pltpu.VMEM((2, 12 * 128, 256), bf16),
-        pltpu.VMEM((9 * 128, 256), bf16),
+        pltpu.VMEM((2, 9 * 128, 256), bf16),
         pltpu.VMEM((16 * COUNT[4], 12 * 128), bf16),
+        pltpu.VMEM((8 * COUNT[4], 256), f32),
         pltpu.VMEM((2 * DIMS, 8, 128), f32),
         pltpu.VMEM((128, 128), f32),
         pltpu.VMEM((8, 128), jnp.int32),
@@ -587,11 +627,11 @@
     out = pl.pallas_call(
         functools.partial(kernel, ns),
         out_shape=jax.ShapeDtypeStruct((rows, 128), f32),
-        in_specs=[vm, vm, sm, sm, sm, sm],
+        in_specs=[hbm] * 6,
         out_specs=vm,
         scratch_shapes=scratch,
         compiler_params=pltpu.CompilerParams(
-            collective_id=0, has_side_effects=True, vmem_limit_bytes=32 << 20
+            collective_id=0, has_side_effects=True, vmem_limit_bytes=58 << 20
         ),
     )(forcing.reshape(rows, 128), fields, coupling.T, jnp.asarray(parent_table()), slot_term, stencil.transpose(1, 2, 0))
     return out.reshape(forcing.shape)

time: 84.6 us -> 79 us (0.934)
  local copies, waits for them, and re-layouts: 5.88 us -> 2.34 us
  Pallas kernels: 78.4 us -> 76.2 us
    unnamed x13 -> x1, local copies, waits for them, and re-layouts: 5.88 us -> 2.34 us
    pallas_call x1, Pallas kernels: 78.4 us -> 76.2 us  [on_device(): pl.pallas_call(functools.partial(kernel, ns), out_shape=jax.ShapeDtypeStr...]
where the time goes in v5:
time: 79 us; the launch traced here: 78.5 us
  Pallas kernels  76.2 us (96%)
  local copies, waits for them, and re-layouts  2.34 us (3%)
    pallas_call x1, Pallas kernels, on_device(): pl.pallas_call(functools.partial(kernel, ns), out_shape=jax.ShapeDtypeStr...  76.2 us
    unnamed x1, local copies, waits for them, and re-layouts  2.34 us

profile of v5, /device:TPU:1, one launch (start us, length us, event | category | flops | bytes accessed | tf_op | source)
XLA Modules:
  0.0 78.5 jit_solution(987452352831113854)
XLA Ops:
  0.0 76.2 %shard_map.64 = f32[2112,128]{1,0:T(8,128)} custom-call(f32[2112,128]{1,0:T(8,128)} %bitcast.5, f32[5,2,32,128]{3,2,1,0:T(8,128)} %refs_1_.1, f32[5,126]{1,0:T(8,128)} %bitcast.7, s32[630]{0:T(1024)} %constant.2.clone.refs_3_, s32[176]{0:T(256)} %refs_4_.1, f32[3,3,27]{2,1,0:T(4,128)} %bitcast.6), custom_call_target="tpu_custom_call" | custom-call | tf_op jit(solution)/shard_map/pallas_call | solution.py:627
  76.2 2.3 %copy.8 = f32[11,3,2,32,128]{4,3,2,1,0:T(8,128)} copy(f32[11,3,2,32,128]{4,3,2,1,0:T(8,128)} %bitcast.4) | data formatting | bytes 2162688

commit v6 on v5

--- a/solution.py
+++ b/solution.py
@@ -23,7 +23,8 @@
 CHUNKS = ((0, 1), (1, 2), (3, 3), (6, 5))
 OUTS = ((0, 1, (0, 1)), (1, 2, (0, 1)), (3, 3, (0, 1)), (6, 5, (0,)), (6, 5, (1,)))
 CHUNK_OF = ((0, 0), (1, 0), (1, 1), (2, 0), (3, 0))
-DIRS = tuple((dx, dz) for dx in (-1, 0, 1) for dz in (-1, 0, 1) if (dx, dz) != (0, 0))
+DIRS = ((-1, -1), (-1, 1), (1, -1), (1, 1), (0, -1), (0, 1), (-1, 0), (1, 0))
+PIECES = ((0, 0, 2), (1, 0, 4), (2, 0, 6), (3, 0, 4), (3, 4, 7), (3, 7, 10))
 MESH = pl.DeviceIdType.MESH
 
 
@@ -129,24 +130,24 @@
         rows_of = jnp.where((i > 0) & (i < GROUPS - 1), 3, 2)
         pl.semaphore_wait(barrier, GROUPS - 1 + sides * rows_of)
 
-    def leaving(c, p, src, dst, s_sem, r_sem, inward):
+    def leaving(c, p, src, dst, s_sem, r_sem, inward, tiles):
         i2 = (i + p) % GROUPS
         k2 = term_of(i2)
         return pltpu.make_async_remote_copy(
-            src_ref=src.at[i2 if inward else k2],
-            dst_ref=dst.at[k if inward else i],
+            src_ref=src.at[i2 if inward else k2, tiles],
+            dst_ref=dst.at[k if inward else i, tiles],
             send_sem=s_sem.at[c, p],
             recv_sem=r_sem.at[c, p],
             device_id={"terms": k2},
             device_id_type=MESH,
         )
 
-    def arriving(c, p, src, dst, s_sem, r_sem, inward):
+    def arriving(c, p, src, dst, s_sem, r_sem, inward, tiles):
         i2 = (i - p + GROUPS) % GROUPS
         k2 = term_of(i2)
         return pltpu.make_async_remote_copy(
-            src_ref=src.at[0],
-            dst_ref=dst.at[k2 if inward else i2],
+            src_ref=src.at[0, tiles],
+            dst_ref=dst.at[k2 if inward else i2, tiles],
             send_sem=s_sem.at[c, p],
             recv_sem=r_sem.at[c, p],
             device_id={"terms": k2},
@@ -160,19 +161,29 @@
 
         lax.fori_loop(1, GROUPS, one, 0)
 
-    def send_in(c):
-        over_peers(lambda p: leaving(c, p, sb[c], rb[c], in_s, in_r, True).start())
-        rb[c][k] = sb[c][i]
+    def piece_in(n):
+        c, lo, hi = PIECES[n]
+        return (sb[c], rb[c], in_s, in_r, True, slice(lo, hi))
+
+    def send_in(n):
+        c, lo, hi = PIECES[n]
+        over_peers(lambda p: leaving(n, p, *piece_in(n)).start())
+        rb[c][k, lo:hi] = sb[c][i, lo:hi]
 
     def wait_in(c):
-        over_peers(lambda p: arriving(c, p, sb[c], rb[c], in_s, in_r, True).wait_recv())
+        for n, piece in enumerate(PIECES):
+            if piece[0] == c:
+                over_peers(lambda p: arriving(n, p, *piece_in(n)).wait_recv())
+
+    def whole_out(c):
+        return (ob[c], qb[c], out_s, out_r, False, slice(0, ob[c].shape[1]))
 
     def send_out(c):
-        over_peers(lambda p: leaving(c, p, ob[c], qb[c], out_s, out_r, False).start())
+        over_peers(lambda p: leaving(c, p, *whole_out(c)).start())
         qb[c][i] = ob[c][k]
 
     def wait_out(c):
-        over_peers(lambda p: arriving(c, p, ob[c], qb[c], out_s, out_r, False).wait_recv())
+        over_peers(lambda p: arriving(c, p, *whole_out(c)).wait_recv())
 
     fetch[0].wait()
     pack(0)
@@ -441,8 +452,6 @@
         c, j0 = CHUNK_OF[lv]
         if lv == 0 or c != CHUNK_OF[lv - 1][0]:
             wait_in(c)
-        if lv == 0:
-            send_in(2)
 
         def load_of(t):
             q = pos[0, START[lv] + t]
@@ -470,10 +479,7 @@
         for part in PARTS[lv]:
             by_five(part, load_of)
             started.append(start_exchange(2 * lv, load_buf[lv], part))
-        if pending:
-            pending.pop()()
-        if lv == 1:
-            send_in(3)
+        ready = pending.pop()() if pending else None
 
         def deliver_to(o, j0, layers, lv=lv):
             def deliver(g, _):
@@ -517,28 +523,34 @@
 
         if WIDE[lv]:
             end_exchange(*started[0])
+            send_in(2 + lv)
+            if ready is not None:
+                send_out(ready)
             settle_wide(lv)
             spread_rim(2 * lv + 1, sett_buf[lv], PARTS[lv][0])
             apply(sett_buf[lv], PARTS[lv][0], 1, image)
 
             def finish(lv=lv, c=c, j0=j0, deliver_to=deliver_to):
                 deliver_to(c, j0, (0, 1))
-                if CHUNK_OF[lv + 1][0] != c:
-                    send_out(c)
+                return c if CHUNK_OF[lv + 1][0] != c else None
 
             pending.append(finish)
         elif lv < 4:
             rimmed = []
             for part, args in zip(PARTS[lv], started):
                 end_exchange(*args)
+                if part is PARTS[lv][-1]:
+                    send_in(5)
+                    send_out(ready)
                 apply(load_buf[lv], part, 0, settle)
                 by_five(part, face)
                 rimmed.append(start_exchange(2 * lv + 1, sett_buf[lv], part))
             deliver_to(c, j0, (0, 1))
             for part, args in zip(PARTS[lv], rimmed):
                 end_exchange(*args)
+                if part is PARTS[lv][-1]:
+                    send_out(c)
                 apply(sett_buf[lv], part, 1, image)
-            send_out(c)
         else:
             lo_at = 8 * COUNT[lv]
             for px in range(2):
@@ -573,10 +585,10 @@
 
         lax.fori_loop(0, 2 * n, unpack, 0)
 
-    for c in range(len(CHUNKS)):
-        over_peers(lambda p: leaving(c, p, sb[c], rb[c], in_s, in_r, True).wait_send())
+    for n in range(len(PIECES)):
+        over_peers(lambda p: leaving(n, p, *piece_in(n)).wait_send())
     for c in range(len(OUTS)):
-        over_peers(lambda p: leaving(c, p, ob[c], qb[c], out_s, out_r, False).wait_send())
+        over_peers(lambda p: leaving(c, p, *whole_out(c)).wait_send())
     for q, e, buf, part in exchanges:
         for n, (dx, dz) in enumerate(DIRS):
             pl.when(inside(dx, dz))(lambda n=n: halo_copy(q, n, e, buf, part).wait_send())
@@ -622,11 +634,11 @@
         pltpu.SMEM((8, 128), jnp.int32),
         dma(()),
     ]
-    scratch += [dma((len(CHUNKS), GROUPS)) for _ in range(2)]
+    scratch += [dma((len(PIECES), GROUPS)) for _ in range(2)]
     scratch += [dma((len(OUTS), GROUPS)) for _ in range(2)] + [dma((9, 8)) for _ in range(2)]
     out = pl.pallas_call(
         functools.partial(kernel, ns),
-        out_shape=jax.ShapeDtypeStruct((rows, 128), f32),
+        out_shape=pltpu.VMEM((rows, 128), f32),
         in_specs=[hbm] * 6,
         out_specs=vm,
         scratch_shapes=scratch,

time: 79 us -> 76.4 us (0.967)
  local copies, waits for them, and re-layouts: 2.34 us -> 0.98 us
  Pallas kernels: 76.2 us -> 75.3 us
    unnamed x1, local copies, waits for them, and re-layouts: 2.34 us -> 0.98 us
    pallas_call x1, Pallas kernels: 76.2 us -> 75.3 us  [on_device(): pl.pallas_call(functools.partial(kernel, ns), out_shape=pltpu.VMEM((rows,...]
where the time goes in v6:
time: 76.4 us; the launch traced here: 76.3 us
  Pallas kernels  75.3 us (99%)
  local copies, waits for them, and re-layouts  0.98 us (1%)
    pallas_call x1, Pallas kernels, on_device(): pl.pallas_call(functools.partial(kernel, ns), out_shape=pltpu.VMEM((rows,...  75.3 us

profile of v6, /device:TPU:1, one launch (start us, length us, event | category | flops | bytes accessed | tf_op | source)
XLA Modules:
  0.0 76.3 jit_solution(5959979534386052136)
XLA Ops:
  0.0 75.3 %shard_map.64 = f32[2112,128]{1,0:T(8,128)S(1)} custom-call(f32[2112,128]{1,0:T(8,128)} %bitcast.5, f32[5,2,32,128]{3,2,1,0:T(8,128)} %refs_1_.1, f32[5,126]{1,0:T(8,128)} %bitcast.7, s32[630]{0:T(1024)} %constant.2.clone.refs_3_, s32[176]{0:T(256)} %refs_4_.1, f32[3,3,27]{2,1,0:T(4,128)} %bitcast.6), custom_call_target="tpu_custom_call" | custom-call | tf_op jit(solution)/shard_map/pallas_call | solution.py:639
  75.3 1.0 %copy.8 = f32[11,3,2,32,128]{4,3,2,1,0:T(8,128)} copy(f32[11,3,2,32,128]{4,3,2,1,0:T(8,128)S(1)} %bitcast.4) | data formatting | bytes 2162688

commit v7 on v6

--- a/solution.py
+++ b/solution.py
@@ -17,9 +17,8 @@
 CAP = (1, 1, 1, 3, 5)
 BASE = (0, 1, 2, 3, 6)
 T8 = (8, 8, 16, 40, 72)
-STEP = (2, 6, 16, 0, 0)
 PARTS = (((0, 1, 8),), ((0, 5, 8),), ((0, 15, 16),), ((0, 16, 16), (16, 19, 24)), ((0, 32, 32), (32, 38, 40)))
-WIDE = (True, True, True, False, False)
+WIDE = (True, True, True, True, False)
 CHUNKS = ((0, 1), (1, 2), (3, 3), (6, 5))
 OUTS = ((0, 1, (0, 1)), (1, 2, (0, 1)), (3, 3, (0, 1)), (6, 5, (0,)), (6, 5, (1,)))
 CHUNK_OF = ((0, 0), (1, 0), (1, 1), (2, 0), (3, 0))
@@ -308,8 +307,8 @@
                 dst = buf.at[tx : tx + 2, t0 : t0 + count, 8:16, :]
             else:
                 side = 1 if dz > 0 else 0
-                src = faces[e].at[side]
-                dst = rims[e].at[1 - side, 1 - side : 3 - side, tx : tx + 2]
+                src = faces[e].at[side, :, :, t0 : t0 + n8]
+                dst = rims[e].at[1 - side, 1 - side : 3 - side, tx : tx + 2, t0 : t0 + n8]
         elif dz == 0:
             src = buf.at[sx, t0 : t0 + count, 8:16, :]
             dst = buf.at[tx, t0 : t0 + count, 8:16, :]
@@ -382,8 +381,9 @@
         both = dot(xs[at : at + rows, 384 * px : 384 * px + 1152], wc[which])
         return both[:, 0:128] + both[:, 128:256]
 
-    def settle_wide(lv):
-        src, rim, step, t8 = load_buf[lv], rims[2 * lv], STEP[lv], T8[lv]
+    def settle_wide(lv, part):
+        t0, count, t8 = part
+        src, rim, step = load_buf[lv], rims[2 * lv], (count + 1) // 2 * 2
         base = 16 * step
         rows = base + 4 * t8
 
@@ -396,7 +396,7 @@
             for dz in range(3):
                 for w in range(4):
                     for b in range(2):
-                        v = [src[2 * b + w, 2 * u + h, 7 + dz : 15 + dz, :] for h in range(2)]
+                        v = [src[2 * b + w, t0 + 2 * u + h, 7 + dz : 15 + dz, :] for h in range(2)]
                         put(b * 8 * step + u * 16, (w * 3 + dz) * 128, jnp.concatenate(v, axis=0))
             return 0
 
@@ -404,7 +404,7 @@
         for side in range(2):
             for dz in range(3):
                 for w in range(4):
-                    v = [rim[side, dz, 2 * b + w] for b in range(2)]
+                    v = [rim[side, dz, 2 * b + w, t0 : t0 + t8] for b in range(2)]
                     put(base + side * 2 * t8, (w * 3 + dz) * 128, jnp.concatenate(v, axis=0))
         res = product(rows, 0)
         one, zero = jnp.float32(1.0), jnp.float32(0.0)
@@ -414,13 +414,13 @@
             b, mine = x // 2, res[x % 2]
             v = mine[b * 8 * step : (b + 1) * 8 * step].reshape(step, 8, 128)
             if x in (1, 2):
-                own_buf[lv][x - 1, 0:step] = v
+                own_buf[lv][x - 1, t0 : t0 + step] = v
             else:
                 v = v * in_x[x]
-            sett_buf[lv][x, 0:step, 8:16, :] = v
+            sett_buf[lv][x, t0 : t0 + step, 8:16, :] = v
             for side in range(2):
                 row = base + side * 2 * t8 + b * t8
-                rims[2 * lv + 1][side, x] = mine[row : row + t8] * (in_x[x] * in_z[side])
+                rims[2 * lv + 1][side, x, t0 : t0 + t8] = mine[row : row + t8] * (in_x[x] * in_z[side])
 
     def stage_rows(src, part, lo_at, at=0):
         t0, count, _ = part
@@ -509,49 +509,27 @@
 
             lax.fori_loop(0, GROUPS, deliver, 0)
 
-        def face(t):
-            for x in range(2):
-                faces[2 * lv + 1][0, x, pl.ds(t, 1), :] = sett_buf[lv][1 + x, t, 8:9, :]
-                faces[2 * lv + 1][1, x, pl.ds(t, 1), :] = sett_buf[lv][1 + x, t, 15:16, :]
-
-        def settle(px, t0, v):
-            own_buf[lv][px, t0 : t0 + v.shape[0]] = v
-            sett_buf[lv][1 + px, t0 : t0 + v.shape[0], 8:16, :] = v
-
         def image(px, t0, v):
             img_buf[lv][px, t0 : t0 + v.shape[0]] = v
 
         if WIDE[lv]:
-            end_exchange(*started[0])
-            send_in(2 + lv)
-            if ready is not None:
-                send_out(ready)
-            settle_wide(lv)
-            spread_rim(2 * lv + 1, sett_buf[lv], PARTS[lv][0])
-            apply(sett_buf[lv], PARTS[lv][0], 1, image)
+            for part, args in zip(PARTS[lv], started):
+                end_exchange(*args)
+                if part is PARTS[lv][-1]:
+                    send_in(2 + lv)
+                    if ready is not None:
+                        send_out(ready)
+                settle_wide(lv, part)
+                spread_rim(2 * lv + 1, sett_buf[lv], part)
+                apply(sett_buf[lv], part, 1, image)
 
             def finish(lv=lv, c=c, j0=j0, deliver_to=deliver_to):
                 deliver_to(c, j0, (0, 1))
                 return c if CHUNK_OF[lv + 1][0] != c else None
 
             pending.append(finish)
-        elif lv < 4:
-            rimmed = []
-            for part, args in zip(PARTS[lv], started):
-                end_exchange(*args)
-                if part is PARTS[lv][-1]:
-                    send_in(5)
-                    send_out(ready)
-                apply(load_buf[lv], part, 0, settle)
-                by_five(part, face)
-                rimmed.append(start_exchange(2 * lv + 1, sett_buf[lv], part))
-            deliver_to(c, j0, (0, 1))
-            for part, args in zip(PARTS[lv], rimmed):
-                end_exchange(*args)
-                if part is PARTS[lv][-1]:
-                    send_out(c)
-                apply(sett_buf[lv], part, 1, image)
         else:
+            send_out(ready)
             lo_at = 8 * COUNT[lv]
             for px in range(2):
                 for part, args in zip(PARTS[lv], started):
@@ -635,7 +613,7 @@
         dma(()),
     ]
     scratch += [dma((len(PIECES), GROUPS)) for _ in range(2)]
-    scratch += [dma((len(OUTS), GROUPS)) for _ in range(2)] + [dma((9, 8)) for _ in range(2)]
+    scratch += [dma((len(OUTS), GROUPS)) for _ in range(2)] + [dma((sum(map(len, PARTS)), 8)) for _ in range(2)]
     out = pl.pallas_call(
         functools.partial(kernel, ns),
         out_shape=pltpu.VMEM((rows, 128), f32),

time: 76.4 us -> 75.9 us (level)
  no operation moved by 1% of the time
where the time goes in v7:
time: 75.9 us; the launch traced here: 75.8 us
  Pallas kernels  74.8 us (99%)
  local copies, waits for them, and re-layouts  0.98 us (1%)
    pallas_call x1, Pallas kernels, on_device(): pl.pallas_call(functools.partial(kernel, ns), out_shape=pltpu.VMEM((rows,...  74.8 us

profile of v7, /device:TPU:1, one launch (start us, length us, event | category | flops | bytes accessed | tf_op | source)
XLA Modules:
  0.0 75.8 jit_solution(14169091074133094416)
XLA Ops:
  0.0 74.8 %shard_map.64 = f32[2112,128]{1,0:T(8,128)S(1)} custom-call(f32[2112,128]{1,0:T(8,128)} %bitcast.5, f32[5,2,32,128]{3,2,1,0:T(8,128)} %refs_1_.1, f32[5,126]{1,0:T(8,128)} %bitcast.7, s32[630]{0:T(1024)} %constant.2.clone.refs_3_, s32[176]{0:T(256)} %refs_4_.1, f32[3,3,27]{2,1,0:T(4,128)} %bitcast.6), custom_call_target="tpu_custom_call" | custom-call | tf_op jit(solution)/shard_map/pallas_call | solution.py:617
  74.8 1.0 %copy.8 = f32[11,3,2,32,128]{4,3,2,1,0:T(8,128)} copy(f32[11,3,2,32,128]{4,3,2,1,0:T(8,128)S(1)} %bitcast.4) | data formatting | bytes 2162688

commit v8 on v7

--- a/solution.py
+++ b/solution.py
@@ -17,7 +17,7 @@
 CAP = (1, 1, 1, 3, 5)
 BASE = (0, 1, 2, 3, 6)
 T8 = (8, 8, 16, 40, 72)
-PARTS = (((0, 1, 8),), ((0, 5, 8),), ((0, 15, 16),), ((0, 16, 16), (16, 19, 24)), ((0, 32, 32), (32, 38, 40)))
+PARTS = (((0, 1, 8),), ((0, 5, 8),), ((0, 15, 16),), ((0, 8, 8), (8, 8, 8), (16, 19, 24)), ((0, 24, 24), (24, 24, 24), (48, 22, 24)))
 WIDE = (True, True, True, True, False)
 CHUNKS = ((0, 1), (1, 2), (3, 3), (6, 5))
 OUTS = ((0, 1, (0, 1)), (1, 2, (0, 1)), (3, 3, (0, 1)), (6, 5, (0,)), (6, 5, (1,)))
@@ -331,7 +331,7 @@
 
     def by_five(part, fn):
         t0, count, _ = part
-        w = next(w for w in (5, 4, 1) if count % w == 0) if count != 19 and count != 38 else 19
+        w = next(w for w in (19, 12, 11, 8, 5, 1) if count % w == 0)
 
         def some(u, _):
             for v in range(w):

time: 75.9 us -> 74.9 us (0.987)
  Pallas kernels: 74.8 us -> 73.3 us
    pallas_call x1, Pallas kernels: 74.8 us -> 73.3 us  [on_device(): pl.pallas_call(functools.partial(kernel, ns), out_shape=pltpu.VMEM((rows,...]
where the time goes in v8:
time: 74.9 us; the launch traced here: 74.3 us
  Pallas kernels  73.3 us (98%)
  local copies, waits for them, and re-layouts  0.98 us (1%)
    pallas_call x1, Pallas kernels, on_device(): pl.pallas_call(functools.partial(kernel, ns), out_shape=pltpu.VMEM((rows,...  73.3 us

profile of v8, /device:TPU:1, one launch (start us, length us, event | category | flops | bytes accessed | tf_op | source)
XLA Modules:
  0.0 74.3 jit_solution(7793807004128123779)
XLA Ops:
  0.0 73.3 %shard_map.64 = f32[2112,128]{1,0:T(8,128)S(1)} custom-call(f32[2112,128]{1,0:T(8,128)} %bitcast.5, f32[5,2,32,128]{3,2,1,0:T(8,128)} %refs_1_.1, f32[5,126]{1,0:T(8,128)} %bitcast.7, s32[630]{0:T(1024)} %constant.2.clone.refs_3_, s32[176]{0:T(256)} %refs_4_.1, f32[3,3,27]{2,1,0:T(4,128)} %bitcast.6), custom_call_target="tpu_custom_call" | custom-call | tf_op jit(solution)/shard_map/pallas_call | solution.py:617
  73.3 1.0 %copy.8 = f32[11,3,2,32,128]{4,3,2,1,0:T(8,128)} copy(f32[11,3,2,32,128]{4,3,2,1,0:T(8,128)S(1)} %bitcast.4) | data formatting | bytes 2162688

commit v9 on v8

--- a/solution.py
+++ b/solution.py
@@ -543,7 +543,18 @@
                 deliver_packed(3 + px, px)
                 send_out(3 + px)
 
+    def sent_early():
+        for n in range(len(PIECES)):
+            over_peers(lambda p: leaving(n, p, *piece_in(n)).wait_send())
+        for c in range(3):
+            over_peers(lambda p: leaving(c, p, *whole_out(c)).wait_send())
+        for q, e, buf, part in exchanges:
+            for n, (dx, dz) in enumerate(DIRS):
+                pl.when(inside(dx, dz))(lambda n=n: halo_copy(q, n, e, buf, part).wait_send())
+
     for c, (j0, n, layers) in enumerate(OUTS):
+        if c == 3:
+            sent_early()
         wait_out(c)
         if len(layers) == 1:
             for m in range(4):
@@ -563,13 +574,8 @@
 
         lax.fori_loop(0, 2 * n, unpack, 0)
 
-    for n in range(len(PIECES)):
-        over_peers(lambda p: leaving(n, p, *piece_in(n)).wait_send())
-    for c in range(len(OUTS)):
+    for c in range(3, len(OUTS)):
         over_peers(lambda p: leaving(c, p, *whole_out(c)).wait_send())
-    for q, e, buf, part in exchanges:
-        for n, (dx, dz) in enumerate(DIRS):
-            pl.when(inside(dx, dz))(lambda n=n: halo_copy(q, n, e, buf, part).wait_send())
 
 
 def on_device(ns, forcing, stencil, fields, coupling, slot_term):

time: 74.9 us -> 73.9 us (0.987)
  Pallas kernels: 73.3 us -> 72.3 us
    pallas_call x1, Pallas kernels: 73.3 us -> 72.3 us  [on_device(): pl.pallas_call(functools.partial(kernel, ns), out_shape=pltpu.VMEM((rows,...]
where the time goes in v9:
time: 73.9 us; the launch traced here: 73.3 us
  Pallas kernels  72.3 us (98%)
  local copies, waits for them, and re-layouts  0.98 us (1%)
    pallas_call x1, Pallas kernels, on_device(): pl.pallas_call(functools.partial(kernel, ns), out_shape=pltpu.VMEM((rows,...  72.3 us

profile of v9, /device:TPU:1, one launch (start us, length us, event | category | flops | bytes accessed | tf_op | source)
XLA Modules:
  0.0 73.3 jit_solution(16408096196988413594)
XLA Ops:
  0.0 72.3 %shard_map.64 = f32[2112,128]{1,0:T(8,128)S(1)} custom-call(f32[2112,128]{1,0:T(8,128)} %bitcast.5, f32[5,2,32,128]{3,2,1,0:T(8,128)} %refs_1_.1, f32[5,126]{1,0:T(8,128)} %bitcast.7, s32[630]{0:T(1024)} %constant.2.clone.refs_3_, s32[176]{0:T(256)} %refs_4_.1, f32[3,3,27]{2,1,0:T(4,128)} %bitcast.6), custom_call_target="tpu_custom_call" | custom-call | tf_op jit(solution)/shard_map/pallas_call | solution.py:623
  72.3 1.0 %copy.8 = f32[11,3,2,32,128]{4,3,2,1,0:T(8,128)} copy(f32[11,3,2,32,128]{4,3,2,1,0:T(8,128)S(1)} %bitcast.4) | data formatting | bytes 2162688

commit v10 on v9

--- a/solution.py
+++ b/solution.py
@@ -287,13 +287,7 @@
         pl.when(i == 0)(lambda: edge(0))
         pl.when(i == GROUPS - 1)(lambda: edge(1))
 
-    for lv in range(5):
-        zero_outside(load_buf[lv], rims[2 * lv], COUNT[lv], WIDE[lv])
-        if lv < 4 and not WIDE[lv]:
-            zero_outside(sett_buf[lv], rims[2 * lv + 1], COUNT[lv], False)
-
-    pack(2)
-    pack(3)
+
     to_smem.wait()
 
     def halo_copy(q, n, e, buf, part):
@@ -479,6 +473,9 @@
         for part in PARTS[lv]:
             by_five(part, load_of)
             started.append(start_exchange(2 * lv, load_buf[lv], part))
+        zero_outside(load_buf[lv], rims[2 * lv], COUNT[lv], WIDE[lv])
+        if lv < 2:
+            pack(2 + lv)
         ready = pending.pop()() if pending else None
 
         def deliver_to(o, j0, layers, lv=lv):

time: 73.9 us -> 73.8 us (level)
  no operation moved by 1% of the time
where the time goes in v10:
time: 73.8 us; the launch traced here: 73.3 us
  Pallas kernels  72.3 us (98%)
  local copies, waits for them, and re-layouts  0.98 us (1%)
    pallas_call x1, Pallas kernels, on_device(): pl.pallas_call(functools.partial(kernel, ns), out_shape=pltpu.VMEM((rows,...  72.3 us

profile of v10, /device:TPU:1, one launch (start us, length us, event | category | flops | bytes accessed | tf_op | source)
XLA Modules:
  0.0 73.3 jit_solution(10193961213377546636)
XLA Ops:
  0.0 72.3 %shard_map.64 = f32[2112,128]{1,0:T(8,128)S(1)} custom-call(f32[2112,128]{1,0:T(8,128)} %bitcast.5, f32[5,2,32,128]{3,2,1,0:T(8,128)} %refs_1_.1, f32[5,126]{1,0:T(8,128)} %bitcast.7, s32[630]{0:T(1024)} %constant.2.clone.refs_3_, s32[176]{0:T(256)} %refs_4_.1, f32[3,3,27]{2,1,0:T(4,128)} %bitcast.6), custom_call_target="tpu_custom_call" | custom-call | tf_op jit(solution)/shard_map/pallas_call | solution.py:620
  72.3 1.0 %copy.8 = f32[11,3,2,32,128]{4,3,2,1,0:T(8,128)} copy(f32[11,3,2,32,128]{4,3,2,1,0:T(8,128)S(1)} %bitcast.4) | data formatting | bytes 2162688
